TPU v7x, 32 devices: a whole 2x2x4 slice. The times are simulated.
32 devices in a mesh: groups: 2 (over y), fsdp: 2 (over core), ep: 8 (over z, x).
Axes of the slice: x: 2, y: 2, z: 4, core: 2. Of those that a mesh axis runs over, the one named last changes fastest.
Arguments:
- tokens: bfloat16 [32, 7168], P(('groups', 'fsdp', 'ep')), parts along dimension 0, may hold values from -6 to 6
- gate_weight: bfloat16 [7168, 1024], P('fsdp', 'ep'), may hold values from -0.0625 to 0.0625
- up_weight: bfloat16 [7168, 1024], P('fsdp', 'ep'), may hold values from -0.0625 to 0.0625
- down_weight: bfloat16 [1024, 7168], P('ep', 'fsdp'), may hold values from -0.1875 to 0.1875
- steering: bfloat16 [1, 7168], replicated, may hold values from -3 to 3
- block_rows: int32 [2, 2, 8], P(None, 'groups'), parts along dimension 1, may hold values from 0 to 7, as said below
- block_gates: float32 [2, 2, 8], P(None, 'groups'), parts along dimension 1, may hold values from 0 to 1, as said below
Outputs:
- mixed: bfloat16 [32, 7168], P(('groups', 'fsdp', 'ep')), parts along dimension 0
There are 2 independent parts, one for each index of `groups`. A program takes and returns all parts, laid end to end along the dimension named above; an argument that names none is the same for every part. Nothing has to cross between parts.
Inputs may be any that keep to these rules, and one draw needn't show every extreme that they name: `block_rows`: within one block the 8 token numbers are distinct. `block_gates`: in each block the gates are positive and falling on the first slots and zero on the rest; in each half one block has no zero gate.
All inputs are finite; a program needn't handle non-finite values.
Results may differ from a plain program's by a relative error of at most 0.0049.
Values may be sent and summed in bfloat16 or wider, within the bound.
No kernel may reach another device: no remote copies, remote signals or barrier semaphores. Data moves between devices by JAX's collectives and lax.ppermute only.
A program may use at most 64 MiB of HBM per device.

v0:
```python
import jax
import jax.numpy as jnp
from jax import lax
from jax.sharding import PartitionSpec as P


def body(tokens, gate_weight, up_weight, down_weight, steering, block_rows, block_gates):
    tok_rows = lax.all_gather(tokens, "ep", axis=0, tiled=True)
    slice_units = gate_weight.shape[1]
    window_experts = block_rows.shape[1]
    ep_count = lax.axis_size("ep")
    window_width = ep_count * slice_units // window_experts
    group_size = window_width // slice_units
    position = lax.axis_index("ep")
    expert = position // group_size
    member = position % group_size
    half_index = lax.axis_index("fsdp")
    expert_rows = lax.dynamic_index_in_dim(block_rows, expert, 1, keepdims=False)
    expert_gates = lax.dynamic_index_in_dim(block_gates, expert, 1, keepdims=False)
    slot_rows = lax.dynamic_index_in_dim(expert_rows, half_index, 0, keepdims=False)
    slot_gates = lax.dynamic_index_in_dim(expert_gates, half_index, 0, keepdims=False)
    picked = jnp.take(tok_rows, slot_rows, axis=0)
    gate_pre = jnp.dot(
        picked,
        lax.all_gather(gate_weight, "fsdp", axis=0, tiled=True),
        preferred_element_type=jnp.float32,
    )
    up_pre = jnp.dot(
        picked,
        lax.all_gather(up_weight, "fsdp", axis=0, tiled=True),
        preferred_element_type=jnp.float32,
    )
    hidden = (jax.nn.silu(gate_pre) * up_pre).astype(jnp.bfloat16)
    half_rows = tok_rows.shape[0]
    width_all = tok_rows.shape[1]
    steer_row = lax.dynamic_index_in_dim(steering, expert, 0, keepdims=False).astype(jnp.float32)
    projected = jnp.dot(
        hidden,
        lax.all_gather(down_weight, "fsdp", axis=1, tiled=True),
        preferred_element_type=jnp.float32,
    )
    leader = (member == 0).astype(jnp.float32)
    weighted = slot_gates[:, None] * (projected + leader * steer_row[None, :])
    partial_sum = jnp.zeros((half_rows, width_all), jnp.float32).at[slot_rows].add(weighted)
    summed = lax.psum_scatter(partial_sum, "ep", scatter_dimension=0, tiled=True)
    return summed.astype(jnp.bfloat16)


def solution(mesh):
    placed = (
        P(("groups", "fsdp", "ep"), None),
        P("fsdp", "ep"),
        P("fsdp", "ep"),
        P("ep", "fsdp"),
        P(),
        P(None, "groups", None),
        P(None, "groups", None),
    )
    return jax.shard_map(
        body,
        mesh=mesh,
        in_specs=placed,
        out_specs=P(("groups", "fsdp", "ep"), None),
        check_vma=False,
    )
```

profile of v0, /device:TPU:0, one launch (start us, length us, event | category | flops | bytes accessed | tf_op | source)
XLA Modules:
  0.0 99.3 jit_solution(15042454936637568538)
XLA Ops:
  6.5 0.0 copy-start
  6.5 0.0 copy-start.3
  6.5 0.0 copy-start.2
  6.5 0.0 all-gather.5.cloned.1.call-start
  6.5 0.7 all-gather.5.cloned.1.call-update
  7.3 0.0 copy-start.4
  7.3 0.0 copy-start.1
  7.3 0.0 all-gather.7.cloned.1.call-start
  7.3 0.7 all-gather.7.cloned.1.call-update
  8.0 0.0 all-gather.9.cloned.1.call-start
  8.1 0.7 all-gather.9.cloned.1.call-update
  8.8 0.0 copy-done.3
  8.9 0.0 copy-done.2
  8.9 32.5 %all-gather = bf16[8,1,7168]{2,1,0:T(2,128)(2,1)S(1)} all-gather(bf16[1,1,7168]{2,1,0:T(2,128)(2,1)S(1)} %bitcast.19), channel_id=1, replica_groups=mesh['groups'=2,'fsdp'=2,'ep'=8] {'ep'}, dimensions={0}, use_global_device_ids=true | all-gather | bytes 129024 | tf_op jit(solution)/shard_map/all_gather | solution.py:8
  41.4 0.0 copy-done
  41.4 0.6 gather_fusion
  42.0 0.0 copy-done.4
  42.1 0.6 dynamic-slice.2
  42.6 0.0 copy-done.1
  42.7 0.0 all-gather.5.cloned.1.call-done
  42.7 2.0 %fusion.4 = f32[8,128]{1,0:T(8,128)S(1)} fusion(bf16[7168,128]{1,0:T(8,128)(2,1)} %all-gather.5.cloned.1.call-done, bf16[8,7168]{1,0:T(8,128)(2,1)S(1)} %gather_fusion, pred[8]{0:T(512)(128)(4,1)S(1)} %compare_and_fusion), kind=kOutput, calls=%fused_computation.10 | convolution fusion | flops 14737408 | bytes 1953800 | tf_op jit(solution)/shard_map/dot_general | solution.py:23
  44.7 0.0 all-gather.7.cloned.1.call-done
  44.8 2.9 %all-gather.9.cloned.1.call-done = bf16[128,7168]{1,0:T(8,128)(2,1)} async-done(((bf16[128,3584]{1,0:T(8,128)(2,1)}), bf16[128,7168]{1,0:T(8,128)(2,1)}) %all-gather.9.cloned.1.call-update) | async-done | bytes 1835024 | tf_op jit(solution)/shard_map/all_gather | solution.py:39
  47.7 2.8 %fusion = f32[8,7168]{1,0:T(8,128)S(1)} fusion(bf16[128,7168]{1,0:T(8,128)(2,1)} %all-gather.9.cloned.1.call-done, bf16[7168,128]{1,0:T(8,128)(2,1)} %all-gather.7.cloned.1.call-done, f32[7168]{0:T(1024)S(1)} %bitcast.18, f32[8]{0:T(128)S(1)} %dynamic-slice_bitcast_fusion, bf16[8,7168]{1,0:T(8,128)(2,1)S(1)} %gather_fusion, ...), kind=kOutput, calls=%fused_computation.3 | convolution fusion | flops 29538304 | bytes 4046888 | tf_op jit(solution)/shard_map/dot_general | solution.py:37
  50.5 0.9 scatter_custom_fusion
  51.4 40.1 %all-reduce.2 = bf16[8,7168]{1,0:T(8,128)(2,1)S(1)} all-reduce(f32[8,7168]{1,0:T(8,128)S(1)} %scatter_custom_fusion), channel_id=2, replica_groups=mesh['groups'=2,'fsdp'=2,'ep'=8] {'ep'}, use_global_device_ids=true, to_apply=%region_1.2.clone | all-reduce | flops 57344 | bytes 344064
  91.5 1.2 %dynamic-slice_convert_fusion = bf16[1,7168]{1,0:T(2,128)(2,1)} fusion(bf16[8,7168]{1,0:T(8,128)(2,1)S(1)} %all-reduce.2, u32[]{:T(128)} %bitcast.6), kind=kLoop, calls=%fused_computation.11 | loop fusion | bytes 28676 | tf_op jit(solution)/shard_map/convert_element_type | solution.py:46
  (6 shorter events, 0.1 us)
Async XLA Ops:
  6.5 34.9 %copy-start = (f32[2,1,8]{2,1,0:T(1,128)S(1)}, f32[2,1,8]{2,1,0:T(1,128)}, u32[]{:S(2)}) copy-start(f32[2,1,8]{2,1,0:T(1,128)} %param.13) | copy-start | bytes 196
  6.5 2.2 %copy-start.3 = (s32[2,1,8]{2,1,0:T(1,128)S(1)}, s32[2,1,8]{2,1,0:T(1,128)}, u32[]{:S(2)}) copy-start(s32[2,1,8]{2,1,0:T(1,128)} %param.12) | copy-start | bytes 196
  6.5 2.3 %copy-start.2 = (bf16[1,7168]{1,0:T(2,128)(2,1)S(1)}, bf16[1,7168]{1,0:T(2,128)(2,1)}, u32[]{:S(2)}) copy-start(bf16[1,7168]{1,0:T(2,128)(2,1)} %param.7) | copy-start | bytes 43012
  6.5 36.1 %all-gather.5.cloned.1.call-start = ((), (), s32[]{:S(2)}) async-start(), calls=%async_computation | async-start | bytes 2752512 | tf_op jit(solution)/shard_map/all_gather | solution.py:25
  7.3 34.8 %copy-start.4 = (u32[32]{0:T(128)S(1)}, u32[32]{0:T(128)}, u32[]{:S(2)}) copy-start(u32[32]{0:T(128)} %constant.79) | copy-start | bytes 388
  7.3 35.4 %copy-start.1 = (bf16[1,7168]{1,0:T(2,128)(2,1)S(1)}, bf16[1,7168]{1,0:T(2,128)(2,1)}, u32[]{:S(2)}) copy-start(bf16[1,7168]{1,0:T(2,128)(2,1)} %param.11) | copy-start | bytes 43012
  7.3 37.5 %all-gather.7.cloned.1.call-start = ((), (), s32[]{:S(2)}) async-start(), calls=%async_computation.1 | async-start | bytes 2752512 | tf_op jit(solution)/shard_map/all_gather | solution.py:30
  8.0 39.7 %all-gather.9.cloned.1.call-start = ((), (), s32[]{:S(2)}) async-start(), calls=%async_computation.2 | async-start | bytes 2752512 | tf_op jit(solution)/shard_map/all_gather | solution.py:39
Sparse Core Ops, SparseCore 0:
  8.9 12.8 all-gather.4
  23.4 11.3 all-gather.6
  36.3 11.3 all-gather.8
where the time goes:
time: 99.5 us; the launch traced here: 99.3 us
  blocking collectives  72.6 us (73%)
  between operations  13.3 us (13%)
  waiting for transfers between devices  5.06 us (5%)
  matrix products  4.84 us (5%)
  local copies, waits for them, and re-layouts  2.47 us (2%)
    unnamed x1, blocking collectives  40.1 us
    all_gather x1, blocking collectives, body(): tok_rows = lax.all_gather(tokens, 'ep', axis=0, tiled=True)  32.5 us
    all_gather x1, waiting for transfers between devices, body(): lax.all_gather(down_weight, 'fsdp', axis=1, tiled=True)  2.95 us
    dot_general x1, matrix products, body(): jnp.dot(hidden, lax.all_gather(down_weight, 'fsdp', axis=1, tiled=True),...  2.79 us
    unnamed x3, waiting for transfers between devices  2.08 us
    dot_general x1, matrix products, body(): jnp.dot(picked, lax.all_gather(gate_weight, 'fsdp', axis=0, tiled=True),...  2.05 us
  transfers between devices with their start and end apart: 3, of which 1 were waited for; matrix products, arithmetic and copies ran while one was open for 3% of the time, Pallas kernels for 0%

commit v1 on v0

v1 whole, which is shorter than its diff:
```python
import jax
import jax.numpy as jnp
from jax import lax
from jax.sharding import PartitionSpec as P


def partner(x, axis, distance):
    count = lax.axis_size(axis)
    return lax.ppermute(x, axis, [(i, i ^ distance) for i in range(count)])


def distances(count):
    found = []
    step = count // 2
    while step:
        found.append(step)
        step //= 2
    return found


def gather_rows(row, axis):
    rows = row
    owners = [0]
    for d in distances(lax.axis_size(axis)):
        rows = jnp.concatenate([rows, partner(rows, axis, d)], axis=0)
        owners = owners + [o ^ d for o in owners]
    return rows, owners


def scatter_sum(rows, axis):
    for d in reversed(distances(lax.axis_size(axis))):
        kept = rows.shape[0] // 2
        got = partner(rows[kept:].astype(jnp.bfloat16), axis, d)
        rows = rows[:kept] + got.astype(jnp.float32)
    return rows


def dot(a, b):
    return jnp.dot(a, b, preferred_element_type=jnp.float32)


def body(tokens, gate_weight, up_weight, down_weight, steering, block_rows, block_gates):
    window_experts = block_rows.shape[1]
    group_size = lax.axis_size("ep") // window_experts
    position = lax.axis_index("ep")
    expert = position // group_size
    half = lax.axis_index("fsdp")
    half_slots = lax.dynamic_index_in_dim(block_rows, half, 0, keepdims=False)
    half_gates = lax.dynamic_index_in_dim(block_gates, half, 0, keepdims=False)

    own_gate = jnp.sum(jnp.where(half_slots == position, half_gates, 0.0), axis=1)
    steer = jnp.sum(own_gate[:, None] * steering.astype(jnp.float32), axis=0, keepdims=True)

    gate_far = partner(gate_weight, "fsdp", 1)
    up_far = partner(up_weight, "fsdp", 1)
    down_far = partner(down_weight, "fsdp", 1)
    rows, owners = gather_rows(tokens, "ep")

    slots = lax.dynamic_index_in_dim(half_slots, expert, 0, keepdims=False)
    gates = lax.dynamic_index_in_dim(half_gates, expert, 0, keepdims=False)
    token = position ^ jnp.asarray(owners)
    token_gate = jnp.sum(jnp.where(slots[None, :] == token[:, None], gates[None, :], 0.0), axis=1, keepdims=True)

    width = tokens.shape[1] // 2
    near = lax.dynamic_slice_in_dim(rows, half * width, width, 1)
    far = lax.dynamic_slice_in_dim(rows, (1 - half) * width, width, 1)
    gate_pre = dot(near, gate_weight) + dot(far, gate_far)
    up_pre = dot(near, up_weight) + dot(far, up_far)
    hidden = (jax.nn.silu(gate_pre) * up_pre).astype(jnp.bfloat16)
    down_near = dot(hidden, down_weight)
    down_other = dot(hidden, down_far)
    first = half == 0
    projected = jnp.concatenate(
        [jnp.where(first, down_near, down_other), jnp.where(first, down_other, down_near)], axis=1
    )
    summed = scatter_sum(token_gate * projected, "ep")
    return (summed + steer).astype(jnp.bfloat16)


def solution(mesh):
    placed = (
        P(("groups", "fsdp", "ep"), None),
        P("fsdp", "ep"),
        P("fsdp", "ep"),
        P("ep", "fsdp"),
        P(),
        P(None, "groups", None),
        P(None, "groups", None),
    )
    return jax.shard_map(
        body,
        mesh=mesh,
        in_specs=placed,
        out_specs=P(("groups", "fsdp", "ep"), None),
        check_vma=False,
    )
```

time: 99.5 us -> 33.1 us (0.33)
  blocking collectives: 72.6 us -> 0 us
  starting transfers between devices: 0.08 us -> 15.6 us
  between operations: 13.3 us -> 0.09 us
  waiting for transfers between devices: 5.06 us -> 9.58 us
  matrix products: 4.84 us -> 1.37 us
  other arithmetic: 0.98 us -> 3.3 us
    unnamed x1 -> x0, blocking collectives: 40.1 us -> none
    all_gather x1 -> x0, blocking collectives: 32.5 us -> none  [body(): tok_rows = lax.all_gather(tokens, 'ep', axis=0, tiled=True)]
    ppermute x0 -> x9, starting transfers between devices: none -> 15.6 us  [partner(): return lax.ppermute(x, axis, [(i, i ^ distance) for i in range(count)])]
    ppermute x0 -> x9, waiting for transfers between devices: none -> 9.58 us  [partner(): return lax.ppermute(x, axis, [(i, i ^ distance) for i in range(count)])]
    dot_general x2 -> x6, matrix products: 4.84 us -> 1.37 us  [dot(): return jnp.dot(a, b, preferred_element_type=jnp.float32)]
    all_gather x3 -> x0, waiting for transfers between devices: 2.98 us -> none  [the longest x1 2.95 us: body(): lax.all_gather(down_weight, 'fsdp', axis=1, tiled=True)]
    unnamed x12 -> x16, local copies, waits for them, and re-layouts: 0.64 us -> 2.84 us
    unnamed x3 -> x0, waiting for transfers between devices: 2.08 us -> none
  transfers between devices with their start and end apart: 3 -> 9, of which waited for: 1 -> 6; matrix products, arithmetic and copies ran while one was open for 3% -> 9% of each run, Pallas kernels for 0% -> 0%
where the time goes in v1:
time: 33.1 us; the launch traced here: 32.9 us
  starting transfers between devices  15.6 us (47%)
  waiting for transfers between devices  9.58 us (29%)
  other arithmetic  3.3 us (10%)
  local copies, waits for them, and re-layouts  2.93 us (9%)
  matrix products  1.37 us (4%)
    ppermute x9, starting transfers between devices, partner(): return lax.ppermute(x, axis, [(i, i ^ distance) for i in range(count)])  15.6 us
    ppermute x9, waiting for transfers between devices, partner(): return lax.ppermute(x, axis, [(i, i ^ distance) for i in range(count)])  9.58 us
    unnamed x16, local copies, waits for them, and re-layouts  2.84 us
    dot_general x6, matrix products, dot(): return jnp.dot(a, b, preferred_element_type=jnp.float32)  1.37 us
    convert_element_type x1, other arithmetic, body(): return (summed + steer).astype(jnp.bfloat16)  1.23 us
    concatenate x3, other arithmetic, gather_rows(): rows = jnp.concatenate([rows, partner(rows, axis, d)], axis=0)  1.13 us
  transfers between devices with their start and end apart: 9, of which 6 were waited for; matrix products, arithmetic and copies ran while one was open for 9% of the time, Pallas kernels for 0%

profile of v1, /device:TPU:0, one launch (start us, length us, event | category | flops | bytes accessed | tf_op | source)
XLA Modules:
  0.0 32.9 jit_solution(688954394087207100)
XLA Ops:
  0.0 4.0 %collective-permute-start = (bf16[1,7168]{1,0:T(2,128)(2,1)}, bf16[1,7168]{1,0:T(2,128)(2,1)S(1)}, u32[]{:S(2)}, u32[]{:S(2)}) collective-permute-start(bf16[1,7168]{1,0:T(2,128)(2,1)} %param.8), channel_id=1, source_target_pairs={{0,4},{1,5},{2,6},{3,7},{4,0},{5,1},{6,2},{7,3},{8,12},{9,13},{10,... | collective-permute-start | bytes 43016 | tf_op jit(solution)/shard_map/ppermute | solution.py:9
  4.0 0.5 %collective-permute-start.4 = (bf16[3584,128]{1,0:T(8,128)(2,1)}, bf16[3584,128]{1,0:T(8,128)(2,1)S(1)}, u32[]{:S(2)}, u32[]{:S(2)}) collective-permute-start(bf16[3584,128]{1,0:T(8,128)(2,1)} %param.10), channel_id=1, source_target_pairs={{0,8},{8,0},{1,9},{9,1},{2,10},{10,2},{3,11},{11,3},{4,12},{12,4},... | collective-permute-start | bytes 2752520 | tf_op jit(solution)/shard_map/ppermute | solution.py:9
  4.6 0.7 %copy-done.7 = s32[8]{0:T(128)S(1)} copy-done((s32[8]{0:T(128)S(1)}, s32[8]{0:T(128)}, u32[]{:S(2)}) %copy-start.7) | copy-done | bytes 56
  5.2 0.9 %collective-permute-done = bf16[1,7168]{1,0:T(2,128)(2,1)S(1)} collective-permute-done((bf16[1,7168]{1,0:T(2,128)(2,1)}, bf16[1,7168]{1,0:T(2,128)(2,1)S(1)}, u32[]{:S(2)}, u32[]{:S(2)}) %collective-permute-start) | collective-permute-done | bytes 14368 | tf_op jit(solution)/shard_map/ppermute | solution.py:9
  6.1 0.9 %pad_maximum_fusion.2 = bf16[2,7168]{1,0:T(2,128)(2,1)S(1)} fusion(bf16[1,7168]{1,0:T(2,128)(2,1)S(1)} %collective-permute-done, bf16[1,7168]{1,0:T(2,128)(2,1)} %param.8), kind=kLoop, calls=%fused_computation.22 | loop fusion | flops 57344 | bytes 57344 | tf_op jit(solution)/shard_map/concatenate | solution.py:25
  7.0 2.0 %collective-permute-start.1 = (bf16[2,7168]{1,0:T(2,128)(2,1)S(1)}, bf16[2,7168]{1,0:T(2,128)(2,1)S(1)}, u32[]{:S(2)}, u32[]{:S(2)}) collective-permute-start(bf16[2,7168]{1,0:T(2,128)(2,1)S(1)} %pad_maximum_fusion.2), channel_id=1, source_target_pairs={{0,2},{1,3},{2,0},{3,1},{4,6},{5,7},{6,4},{7,5},{8,10},{9,11},{10,... | collective-permute-start | bytes 86024 | tf_op jit(solution)/shard_map/ppermute | solution.py:9
  9.0 0.7 %copy-done.6 = f32[2,1,8]{2,1,0:T(1,128)S(1)} copy-done((f32[2,1,8]{2,1,0:T(1,128)S(1)}, f32[2,1,8]{2,1,0:T(1,128)}, u32[]{:S(2)}) %copy-start.6) | copy-done | bytes 88
  9.6 0.6 %fusion.14 = (f32[]{:T(128)}, f32[8]{0:T(128)S(1)}) fusion(s32[]{:T(128)S(6)} %axis_index.25, s32[2,1,8]{2,1,0:T(1,128)S(1)} %copy-done.5, s32[]{:T(128)S(6)} %select_n.48, f32[2,1,8]{2,1,0:T(1,128)S(1)} %copy-done.6), kind=kLoop, calls=%fused_computation.32 | loop fusion | flops 23 | bytes 108 | tf_op jit(solution)/shard_map/reduce_sum | solution.py:51
  10.3 0.7 %collective-permute-done.1 = bf16[2,7168]{1,0:T(2,128)(2,1)S(1)} collective-permute-done((bf16[2,7168]{1,0:T(2,128)(2,1)S(1)}, bf16[2,7168]{1,0:T(2,128)(2,1)S(1)}, u32[]{:S(2)}, u32[]{:S(2)}) %collective-permute-start.1) | collective-permute-done | bytes 28704 | tf_op jit(solution)/shard_map/ppermute | solution.py:9
  10.9 0.1 pad_maximum_fusion.1
  11.0 2.1 %collective-permute-start.2 = (bf16[4,7168]{1,0:T(4,128)(2,1)S(1)}, bf16[4,7168]{1,0:T(4,128)(2,1)S(1)}, u32[]{:S(2)}, u32[]{:S(2)}) collective-permute-start(bf16[4,7168]{1,0:T(4,128)(2,1)S(1)} %pad_maximum_fusion.1), channel_id=1, source_target_pairs={{0,1},{1,0},{2,3},{3,2},{4,5},{5,4},{6,7},{7,6},{8,9},{9,8},{10,11... | collective-permute-start | bytes 172040 | tf_op jit(solution)/shard_map/ppermute | solution.py:9
  13.1 0.2 select_reduce_fusion
  13.3 2.0 %collective-permute-done.2 = bf16[4,7168]{1,0:T(4,128)(2,1)S(1)} collective-permute-done((bf16[4,7168]{1,0:T(4,128)(2,1)S(1)}, bf16[4,7168]{1,0:T(4,128)(2,1)S(1)}, u32[]{:S(2)}, u32[]{:S(2)}) %collective-permute-start.2) | collective-permute-done | bytes 57376 | tf_op jit(solution)/shard_map/ppermute | solution.py:9
  15.3 0.1 pad_maximum_fusion
  15.4 0.0 copy-start
  15.4 0.2 fusion.4
  15.7 0.2 fusion.2
  15.9 0.7 %copy-done = bf16[3584,128]{1,0:T(8,128)(2,1)S(1)} copy-done((bf16[3584,128]{1,0:T(8,128)(2,1)S(1)}, bf16[3584,128]{1,0:T(8,128)(2,1)}, u32[]{:S(2)}) %copy-start) | copy-done | bytes 917528
  16.6 0.2 convolution_add_fusion.1
  16.8 0.1 copy-done.1
  16.9 0.2 fusion.1
  17.2 0.7 %copy-done.2 = bf16[128,3584]{1,0:T(8,128)(2,1)S(1)} copy-done((bf16[128,3584]{1,0:T(8,128)(2,1)S(1)}, bf16[128,3584]{1,0:T(8,128)(2,1)}, u32[]{:S(2)}) %copy-start.2) | copy-done | bytes 917528
  17.9 0.2 fusion.17
  18.1 0.2 broadcast_select_fusion.1
  18.3 0.1 maximum_multiply_fusion
  18.5 2.1 %collective-permute-start.6 = (bf16[4,7168]{1,0:T(4,128)(2,1)S(1)}, bf16[4,7168]{1,0:T(4,128)(2,1)S(1)}, u32[]{:S(2)}, u32[]{:S(2)}) collective-permute-start(bf16[4,7168]{1,0:T(4,128)(2,1)S(1)} %slice.43), channel_id=1, source_target_pairs={{0,1},{1,0},{2,3},{3,2},{4,5},{5,4},{6,7},{7,6},{8,9},{9,8},{10,11... | collective-permute-start | bytes 172040 | tf_op jit(solution)/shard_map/ppermute | solution.py:9
  20.5 2.2 %collective-permute-done.6 = bf16[4,7168]{1,0:T(4,128)(2,1)S(1)} collective-permute-done((bf16[4,7168]{1,0:T(4,128)(2,1)S(1)}, bf16[4,7168]{1,0:T(4,128)(2,1)S(1)}, u32[]{:S(2)}, u32[]{:S(2)}) %collective-permute-start.6) | collective-permute-done | bytes 57376 | tf_op jit(solution)/shard_map/ppermute | solution.py:9
  22.8 2.0 %collective-permute-start.7 = (bf16[2,7168]{1,0:T(2,128)(2,1)S(1)}, bf16[2,7168]{1,0:T(2,128)(2,1)S(1)}, u32[]{:S(2)}, u32[]{:S(2)}) collective-permute-start(bf16[2,7168]{1,0:T(2,128)(2,1)S(1)} %slice.44), channel_id=1, source_target_pairs={{0,2},{1,3},{2,0},{3,1},{4,6},{5,7},{6,4},{7,5},{8,10},{9,11},{10,... | collective-permute-start | bytes 86024 | tf_op jit(solution)/shard_map/ppermute | solution.py:9
  24.7 2.0 %collective-permute-done.7 = bf16[2,7168]{1,0:T(2,128)(2,1)S(1)} collective-permute-done((bf16[2,7168]{1,0:T(2,128)(2,1)S(1)}, bf16[2,7168]{1,0:T(2,128)(2,1)S(1)}, u32[]{:S(2)}, u32[]{:S(2)}) %collective-permute-start.7) | collective-permute-done | bytes 28704 | tf_op jit(solution)/shard_map/ppermute | solution.py:9
  26.8 3.0 %collective-permute-start.8 = (bf16[1,7168]{1,0:T(2,128)(2,1)S(1)}, bf16[1,7168]{1,0:T(2,128)(2,1)S(1)}, u32[]{:S(2)}, u32[]{:S(2)}) collective-permute-start(bf16[1,7168]{1,0:T(2,128)(2,1)S(1)} %slice.45), channel_id=1, source_target_pairs={{0,4},{1,5},{2,6},{3,7},{4,0},{5,1},{6,2},{7,3},{8,12},{9,13},{10,... | collective-permute-start | bytes 43016 | tf_op jit(solution)/shard_map/ppermute | solution.py:9
  29.8 1.9 %collective-permute-done.8 = bf16[1,7168]{1,0:T(2,128)(2,1)S(1)} collective-permute-done((bf16[1,7168]{1,0:T(2,128)(2,1)S(1)}, bf16[1,7168]{1,0:T(2,128)(2,1)S(1)}, u32[]{:S(2)}, u32[]{:S(2)}) %collective-permute-start.8) | collective-permute-done | bytes 14368 | tf_op jit(solution)/shard_map/ppermute | solution.py:9
  31.6 1.2 %fusion.9 = bf16[1,7168]{1,0:T(2,128)(2,1)} fusion(bf16[1,7168]{1,0:T(2,128)(2,1)S(1)} %copy-done.4, bf16[1,7168]{1,0:T(2,128)(2,1)S(1)} %collective-permute-done.8, f32[2,7168]{1,0:T(2,128)S(1)} %slice_add_fusion.1, f32[]{:T(128)} %get-tuple-element.7), kind=kLoop, calls=%fused_computation.23 | loop fusion | flops 43008 | bytes 71684 | tf_op jit(solution)/shard_map/convert_element_type | solution.py:77
  (22 shorter events, 0.2 us)
Async XLA Ops:
  0.0 6.1 %collective-permute-start = (bf16[1,7168]{1,0:T(2,128)(2,1)}, bf16[1,7168]{1,0:T(2,128)(2,1)S(1)}, u32[]{:S(2)}, u32[]{:S(2)}) collective-permute-start(bf16[1,7168]{1,0:T(2,128)(2,1)} %param.8), channel_id=1, source_target_pairs={{0,4},{1,5},{2,6},{3,7},{4,0},{5,1},{6,2},{7,3},{8,12},{9,13},{10,... | collective-permute-start | bytes 43016 | tf_op jit(solution)/shard_map/ppermute | solution.py:9
  4.0 11.4 %collective-permute-start.3 = (bf16[3584,128]{1,0:T(8,128)(2,1)}, bf16[3584,128]{1,0:T(8,128)(2,1)S(1)}, u32[]{:S(2)}, u32[]{:S(2)}) collective-permute-start(bf16[3584,128]{1,0:T(8,128)(2,1)} %param.9), channel_id=1, source_target_pairs={{0,8},{8,0},{1,9},{9,1},{2,10},{10,2},{3,11},{11,3},{4,12},{12,4},... | collective-permute-start | bytes 2752520 | tf_op jit(solution)/shard_map/ppermute | solution.py:9
  4.0 11.6 %collective-permute-start.4 = (bf16[3584,128]{1,0:T(8,128)(2,1)}, bf16[3584,128]{1,0:T(8,128)(2,1)S(1)}, u32[]{:S(2)}, u32[]{:S(2)}) collective-permute-start(bf16[3584,128]{1,0:T(8,128)(2,1)} %param.10), channel_id=1, source_target_pairs={{0,8},{8,0},{1,9},{9,1},{2,10},{10,2},{3,11},{11,3},{4,12},{12,4},... | collective-permute-start | bytes 2752520 | tf_op jit(solution)/shard_map/ppermute | solution.py:9
  4.5 13.5 %collective-permute-start.5 = (bf16[128,3584]{1,0:T(8,128)(2,1)}, bf16[128,3584]{1,0:T(8,128)(2,1)S(1)}, u32[]{:S(2)}, u32[]{:S(2)}) collective-permute-start(bf16[128,3584]{1,0:T(8,128)(2,1)} %param.11), channel_id=1, source_target_pairs={{0,8},{8,0},{1,9},{9,1},{2,10},{10,2},{3,11},{11,3},{4,12},{12,4},... | collective-permute-start | bytes 2752520 | tf_op jit(solution)/shard_map/ppermute | solution.py:9
  4.6 0.7 %copy-start.7 = (s32[8]{0:T(128)S(1)}, s32[8]{0:T(128)}, u32[]{:S(2)}) copy-start(s32[8]{0:T(128)} %constant.50.clone) | copy-start | bytes 100
  5.2 3.8 %copy-start.5 = (s32[2,1,8]{2,1,0:T(1,128)S(1)}, s32[2,1,8]{2,1,0:T(1,128)}, u32[]{:S(2)}) copy-start(s32[2,1,8]{2,1,0:T(1,128)} %param.13) | copy-start | bytes 196
  6.1 4.8 %copy-start.3 = (bf16[1,7168]{1,0:T(2,128)(2,1)S(1)}, bf16[1,7168]{1,0:T(2,128)(2,1)}, u32[]{:S(2)}) copy-start(bf16[1,7168]{1,0:T(2,128)(2,1)} %param.8) | copy-start | bytes 43012
  7.0 3.9 %collective-permute-start.1 = (bf16[2,7168]{1,0:T(2,128)(2,1)S(1)}, bf16[2,7168]{1,0:T(2,128)(2,1)S(1)}, u32[]{:S(2)}, u32[]{:S(2)}) collective-permute-start(bf16[2,7168]{1,0:T(2,128)(2,1)S(1)} %pad_maximum_fusion.2), channel_id=1, source_target_pairs={{0,2},{1,3},{2,0},{3,1},{4,6},{5,7},{6,4},{7,5},{8,10},{9,11},{10,... | collective-permute-start | bytes 86024 | tf_op jit(solution)/shard_map/ppermute | solution.py:9
  9.0 0.7 %copy-start.6 = (f32[2,1,8]{2,1,0:T(1,128)S(1)}, f32[2,1,8]{2,1,0:T(1,128)}, u32[]{:S(2)}) copy-start(f32[2,1,8]{2,1,0:T(1,128)} %param.14) | copy-start | bytes 196
  11.0 4.2 %collective-permute-start.2 = (bf16[4,7168]{1,0:T(4,128)(2,1)S(1)}, bf16[4,7168]{1,0:T(4,128)(2,1)S(1)}, u32[]{:S(2)}, u32[]{:S(2)}) collective-permute-start(bf16[4,7168]{1,0:T(4,128)(2,1)S(1)} %pad_maximum_fusion.1), channel_id=1, source_target_pairs={{0,1},{1,0},{2,3},{3,2},{4,5},{5,4},{6,7},{7,6},{8,9},{9,8},{10,11... | collective-permute-start | bytes 172040 | tf_op jit(solution)/shard_map/ppermute | solution.py:9
  15.4 1.2 %copy-start = (bf16[3584,128]{1,0:T(8,128)(2,1)S(1)}, bf16[3584,128]{1,0:T(8,128)(2,1)}, u32[]{:S(2)}) copy-start(bf16[3584,128]{1,0:T(8,128)(2,1)} %param.9) | copy-start | bytes 2752516
  15.7 1.3 %copy-start.1 = (bf16[3584,128]{1,0:T(8,128)(2,1)S(1)}, bf16[3584,128]{1,0:T(8,128)(2,1)}, u32[]{:S(2)}) copy-start(bf16[3584,128]{1,0:T(8,128)(2,1)} %param.10) | copy-start | bytes 2752516
  16.6 1.2 %copy-start.2 = (bf16[128,3584]{1,0:T(8,128)(2,1)S(1)}, bf16[128,3584]{1,0:T(8,128)(2,1)}, u32[]{:S(2)}) copy-start(bf16[128,3584]{1,0:T(8,128)(2,1)} %param.11) | copy-start | bytes 2752516
  18.5 4.2 %collective-permute-start.6 = (bf16[4,7168]{1,0:T(4,128)(2,1)S(1)}, bf16[4,7168]{1,0:T(4,128)(2,1)S(1)}, u32[]{:S(2)}, u32[]{:S(2)}) collective-permute-start(bf16[4,7168]{1,0:T(4,128)(2,1)S(1)} %slice.43), channel_id=1, source_target_pairs={{0,1},{1,0},{2,3},{3,2},{4,5},{5,4},{6,7},{7,6},{8,9},{9,8},{10,11... | collective-permute-start | bytes 172040 | tf_op jit(solution)/shard_map/ppermute | solution.py:9
  22.8 3.9 %collective-permute-start.7 = (bf16[2,7168]{1,0:T(2,128)(2,1)S(1)}, bf16[2,7168]{1,0:T(2,128)(2,1)S(1)}, u32[]{:S(2)}, u32[]{:S(2)}) collective-permute-start(bf16[2,7168]{1,0:T(2,128)(2,1)S(1)} %slice.44), channel_id=1, source_target_pairs={{0,2},{1,3},{2,0},{3,1},{4,6},{5,7},{6,4},{7,5},{8,10},{9,11},{10,... | collective-permute-start | bytes 86024 | tf_op jit(solution)/shard_map/ppermute | solution.py:9
  26.7 4.9 %copy-start.4 = (bf16[1,7168]{1,0:T(2,128)(2,1)S(1)}, bf16[1,7168]{1,0:T(2,128)(2,1)}, u32[]{:S(2)}) copy-start(bf16[1,7168]{1,0:T(2,128)(2,1)} %param.12) | copy-start | bytes 43012
  26.8 4.8 %collective-permute-start.8 = (bf16[1,7168]{1,0:T(2,128)(2,1)S(1)}, bf16[1,7168]{1,0:T(2,128)(2,1)S(1)}, u32[]{:S(2)}, u32[]{:S(2)}) collective-permute-start(bf16[1,7168]{1,0:T(2,128)(2,1)S(1)} %slice.45), channel_id=1, source_target_pairs={{0,4},{1,5},{2,6},{3,7},{4,0},{5,1},{6,2},{7,3},{8,12},{9,13},{10,... | collective-permute-start | bytes 43016 | tf_op jit(solution)/shard_map/ppermute | solution.py:9

commit v2 on v0

v2 whole, which is shorter than its diff:
```python
import functools

import jax
import jax.numpy as jnp
from jax import lax
from jax.experimental import pallas as pl
from jax.experimental.pallas import tpu as pltpu
from jax.sharding import PartitionSpec as P

VMEM_LIMIT = 48 * 2**20


def swap_cores(x):
    return lax.ppermute(x, "fsdp", [(0, 1), (1, 0)])


def exchange(x, distance, cross):
    count = lax.axis_size("ep")
    pairs = [(f * count + e, (f ^ cross) * count + (e ^ distance)) for f in range(2) for e in range(count)]
    return lax.ppermute(x, ("fsdp", "ep"), pairs)


def stages(count):
    steps = [(1, 2, 1)] if count > 1 else []
    base = 2
    while base < count:
        radix = 4 if base * 4 <= count else 2
        steps.append((base, radix, 1))
        base *= radix
    return steps


def dot(a, b):
    return jnp.dot(a, b, preferred_element_type=jnp.float32)


def stage_kernel(*refs):
    count = len(refs) // 2
    copies = [pltpu.make_async_copy(refs[i], refs[count + i], refs[-1].at[i]) for i in range(count)]
    for copy in copies:
        copy.start()
    for copy in copies:
        copy.wait()


def stage(*arrays):
    return pl.pallas_call(
        stage_kernel,
        out_shape=[jax.ShapeDtypeStruct(a.shape, a.dtype) for a in arrays],
        in_specs=[pl.BlockSpec(memory_space=pltpu.HBM)] * len(arrays),
        out_specs=[pl.BlockSpec(memory_space=pltpu.VMEM)] * len(arrays),
        scratch_shapes=[pltpu.SemaphoreType.DMA((len(arrays),))],
        compiler_params=pltpu.CompilerParams(vmem_limit_bytes=VMEM_LIMIT),
        name="stage",
    )(*[pltpu.with_memory_space_constraint(a, pltpu.HBM) for a in arrays])


def experts_kernel(owners, pieces, *refs):
    row_refs = refs[:pieces]
    gate_ref, up_ref, down_ref, steer_ref, slots_ref, gates_ref, gate_far_ref, up_far_ref, down_far_ref = refs[pieces:pieces + 9]
    keep_ref = refs[pieces + 9]
    send_refs = refs[pieces + 10:2 * pieces + 9]
    rows_scr, out_scr = refs[2 * pieces + 9:]
    window_experts = slots_ref.shape[1]
    position = lax.axis_index("ep")
    half = lax.axis_index("fsdp")
    expert = position // (lax.axis_size("ep") // window_experts)
    count = len(owners)
    chunk = count // pieces
    width = gate_ref.shape[0]
    near = pl.multiple_of(half * width, 128)
    far = pl.multiple_of((1 - half) * width, 128)
    for k, ref in enumerate(row_refs):
        rows_scr[k * chunk:(k + 1) * chunk, :] = ref[...].astype(jnp.float32)
    x_near = rows_scr[:, pl.ds(near, width)].astype(jnp.bfloat16)
    x_far = rows_scr[:, pl.ds(far, width)].astype(jnp.bfloat16)
    gate_pre = dot(x_near, gate_ref[...]) + dot(x_far, gate_far_ref[...])
    up_pre = dot(x_near, up_ref[...]) + dot(x_far, up_far_ref[...])
    hidden = (gate_pre / (1.0 + jnp.exp(-gate_pre)) * up_pre).astype(jnp.bfloat16)
    row = lax.broadcasted_iota(jnp.int32, (count, 1), 0)
    offset = jnp.zeros((count, 1), jnp.int32)
    other = jnp.zeros((count, 1), jnp.int32)
    for j, (o, c) in enumerate(owners):
        if o:
            offset = jnp.where(row == j, o, offset)
        if c:
            other = jnp.where(row == j, 1, other)
    token = position ^ offset
    row_half = half ^ other
    token_gate = jnp.zeros((count, 1), jnp.float32)
    for h in range(2):
        slots = slots_ref[h, pl.ds(expert, 1), :]
        gates = gates_ref[h, pl.ds(expert, 1), :]
        found = jnp.sum(jnp.where(slots == token, gates, 0.0), axis=1, keepdims=True)
        token_gate = jnp.where(row_half == h, found, token_gate)
    out_scr[:, pl.ds(near, width)] = token_gate * dot(hidden, down_ref[...])
    out_scr[:, pl.ds(far, width)] = token_gate * dot(hidden, down_far_ref[...])
    own_gate = jnp.sum(jnp.where(slots_ref[half] == position, gates_ref[half], 0.0), axis=1, keepdims=True)
    steer = jnp.sum(own_gate * steer_ref[...].astype(jnp.float32), axis=0, keepdims=True)
    out_scr[0:1, :] = out_scr[0:1, :] + steer
    keep_ref[...] = out_scr[0:chunk, :]
    for k, ref in enumerate(send_refs):
        ref[...] = out_scr[(k + 1) * chunk:(k + 2) * chunk, :].astype(jnp.bfloat16)


def body(tokens, gate_weight, up_weight, down_weight, steering, block_rows, block_gates):
    count = lax.axis_size("ep")
    width_all = tokens.shape[1]
    here = None
    pieces = [tokens]
    owners = [(0, 0)]
    steps = stages(count)
    for i, (base, radix, cross) in enumerate(steps):
        rows = jnp.concatenate(pieces, axis=0) if len(pieces) > 1 else pieces[0]
        if i == 1:
            here = stage(gate_weight, up_weight, down_weight, steering, block_rows, block_gates)
            rows, here = lax.optimization_barrier((rows, here))
        pieces = [rows] + [exchange(rows, k * base, cross) for k in range(1, radix)]
        owners = [(o ^ (k * base), c ^ (cross if k else 0)) for k in range(radix) for o, c in owners]
    if here is None:
        here = stage(gate_weight, up_weight, down_weight, steering, block_rows, block_gates)
    far = [swap_cores(w) for w in (gate_weight, up_weight, down_weight)]
    chunk = count // len(pieces)
    vmem = pl.BlockSpec(memory_space=pltpu.VMEM)
    outs = pl.pallas_call(
        functools.partial(experts_kernel, owners, len(pieces)),
        out_shape=[jax.ShapeDtypeStruct((chunk, width_all), jnp.float32)]
        + [jax.ShapeDtypeStruct((chunk, width_all), jnp.bfloat16)] * (len(pieces) - 1),
        in_specs=[vmem] * (len(pieces) + 9),
        out_specs=[vmem] * len(pieces),
        scratch_shapes=[pltpu.VMEM((count, width_all), jnp.float32), pltpu.VMEM((count, width_all), jnp.float32)],
        compiler_params=pltpu.CompilerParams(vmem_limit_bytes=VMEM_LIMIT),
        name="experts",
    )(*pieces, *here, *far)
    total, sends = outs[0], list(outs[1:])
    for i, (base, radix, cross) in enumerate(reversed(steps)):
        if i:
            chunk = total.shape[0] // radix
            sends = [total[k * chunk:(k + 1) * chunk].astype(jnp.bfloat16) for k in range(1, radix)]
            total = total[:chunk]
        got = [exchange(s, k * base, cross) for k, s in enumerate(sends, 1)]
        for g in got:
            total = total + g.astype(jnp.float32)
    return total.astype(jnp.bfloat16)


def solution(mesh):
    placed = (
        P(("groups", "fsdp", "ep"), None),
        P("fsdp", "ep"),
        P("fsdp", "ep"),
        P("ep", "fsdp"),
        P(),
        P(None, "groups", None),
        P(None, "groups", None),
    )
    return jax.shard_map(
        body,
        mesh=mesh,
        in_specs=placed,
        out_specs=P(("groups", "fsdp", "ep"), None),
        check_vma=False,
    )
```

time: 99.5 us -> 28.5 us (0.29)
  blocking collectives: 72.6 us -> 0 us
  between operations: 13.3 us -> 0.05 us
  starting transfers between devices: 0.08 us -> 12.9 us
  waiting for transfers between devices: 5.06 us -> 11.7 us
  matrix products: 4.84 us -> 0 us
  Pallas kernels: 0 us -> 2.79 us
  local copies, waits for them, and re-layouts: 2.47 us -> 0.04 us
    unnamed x1 -> x0, blocking collectives: 40.1 us -> none
    all_gather x1 -> x0, blocking collectives: 32.5 us -> none  [body(): tok_rows = lax.all_gather(tokens, 'ep', axis=0, tiled=True)]
    ppermute x0 -> x11, starting transfers between devices: none -> 12.9 us  [the longest x8 12 us: exchange(): return lax.ppermute(x, ('fsdp', 'ep'), pairs)]
    ppermute x0 -> x11, waiting for transfers between devices: none -> 11.7 us  [the longest x8 11.7 us: exchange(): return lax.ppermute(x, ('fsdp', 'ep'), pairs)]
    dot_general x2 -> x0, matrix products: 4.84 us -> none  [the longest x1 2.79 us: body(): jnp.dot(hidden, lax.all_gather(down_weight, 'fsdp', axis=1, tiled=True),...]
    all_gather x3 -> x0, waiting for transfers between devices: 2.98 us -> none  [the longest x1 2.95 us: body(): lax.all_gather(down_weight, 'fsdp', axis=1, tiled=True)]
    pallas_call x0 -> x2, Pallas kernels: none -> 2.79 us  [the longest x1 1.79 us: stage(): pl.pallas_call(stage_kernel, out_shape=[jax.ShapeDtypeStruct(a.shape, a.d...]
    unnamed x3 -> x0, waiting for transfers between devices: 2.08 us -> none
  transfers between devices with their start and end apart: 3 -> 11, of which waited for: 1 -> 6; matrix products, arithmetic and copies ran while one was open for 3% -> 0% of each run, Pallas kernels for 0% -> 6%
where the time goes in v2:
time: 28.5 us; the launch traced here: 28.3 us
  starting transfers between devices  12.9 us (45%)
  waiting for transfers between devices  11.7 us (41%)
  Pallas kernels  2.79 us (10%)
  other arithmetic  0.78 us (3%)
    ppermute x8, starting transfers between devices, exchange(): return lax.ppermute(x, ('fsdp', 'ep'), pairs)  12 us
    ppermute x8, waiting for transfers between devices, exchange(): return lax.ppermute(x, ('fsdp', 'ep'), pairs)  11.7 us
    pallas_call x1, Pallas kernels, stage(): pl.pallas_call(stage_kernel, out_shape=[jax.ShapeDtypeStruct(a.shape, a.d...  1.79 us
    pallas_call x1, Pallas kernels, body(): pl.pallas_call(functools.partial(experts_kernel, owners, len(pieces)), ou...  1 us
    ppermute x3, starting transfers between devices, swap_cores(): return lax.ppermute(x, 'fsdp', [(0, 1), (1, 0)])  0.96 us
    convert_element_type x1, other arithmetic, body(): return total.astype(jnp.bfloat16)  0.65 us
  transfers between devices with their start and end apart: 11, of which 6 were waited for; matrix products, arithmetic and copies ran while one was open for 0% of the time, Pallas kernels for 6%

profile of v2, /device:TPU:0, one launch (start us, length us, event | category | flops | bytes accessed | tf_op | source)
XLA Modules:
  0.0 28.3 jit_solution(14868528057838044425)
XLA Ops:
  0.0 0.0 copy-start
  0.0 0.5 %collective-permute-start.4 = (bf16[3584,128]{1,0:T(8,128)(2,1)}, bf16[3584,128]{1,0:T(8,128)(2,1)S(1)}, u32[]{:S(2)}, u32[]{:S(2)}) collective-permute-start(bf16[3584,128]{1,0:T(8,128)(2,1)} %refs_0_.1), channel_id=1, source_target_pairs={{0,8},{8,0},{1,9},{9,1},{2,10},{10,2},{3,11},{11,3},{4,12},{12,4},... | collective-permute-start | bytes 2752520 | tf_op jit(solution)/shard_map/ppermute | solution.py:14
  0.5 0.1 collective-permute-start.5
  0.5 0.4 %collective-permute-start.6 = (bf16[128,3584]{1,0:T(8,128)(2,1)}, bf16[128,3584]{1,0:T(8,128)(2,1)S(1)}, u32[]{:S(2)}, u32[]{:S(2)}) collective-permute-start(bf16[128,3584]{1,0:T(8,128)(2,1)} %refs_2_.1), channel_id=1, source_target_pairs={{0,8},{8,0},{1,9},{9,1},{2,10},{10,2},{3,11},{11,3},{4,12},{12,4},... | collective-permute-start | bytes 2752520 | tf_op jit(solution)/shard_map/ppermute | solution.py:14
  1.0 2.6 %collective-permute-start = (bf16[1,7168]{1,0:T(2,128)(2,1)}, bf16[1,7168]{1,0:T(2,128)(2,1)S(1)}, u32[]{:S(2)}, u32[]{:S(2)}) collective-permute-start(bf16[1,7168]{1,0:T(2,128)(2,1)} %param.7), channel_id=1, source_target_pairs={{0,9},{1,8},{2,11},{3,10},{4,13},{5,12},{6,15},{7,14},{8,1},{9,0},... | collective-permute-start | bytes 43016 | tf_op jit(solution)/shard_map/ppermute | solution.py:20
  3.6 1.8 %stage.1 = (bf16[3584,128]{1,0:T(8,128)(2,1)S(1)}, bf16[3584,128]{1,0:T(8,128)(2,1)S(1)}, bf16[128,3584]{1,0:T(8,128)(2,1)S(1)}, bf16[1,7168]{1,0:T(2,128)(2,1)S...) custom-call(bf16[3584,128]{1,0:T(8,128)(2,1)} %refs_0_.1, bf16[3584,128]{1,0:T(8,128)(2,1)} %refs_1_.1, ...), custom_call_target="tpu_custom_call" | custom-call | tf_op jit(solution)/shard_map/stage/pallas_call | solution.py:47
  5.4 0.0 collective-permute-done
  5.4 0.0 copy-done
  5.4 0.1 pad_maximum_fusion.refs_0_
  5.5 3.9 %collective-permute-start.3 = (bf16[2,7168]{1,0:T(2,128)(2,1)S(1)}, bf16[2,7168]{1,0:T(2,128)(2,1)S(1)}, u32[]{:S(2)}, u32[]{:S(2)}) collective-permute-start(bf16[2,7168]{1,0:T(2,128)(2,1)S(1)} %pad_maximum_fusion.refs_0_), channel_id=1, source_target_pairs={{0,14},{1,15},{2,12},{3,13},{4,10},{5,11},{6,8},{7,9},{8,6},{9,7},... | collective-permute-start | bytes 86024 | tf_op jit(solution)/shard_map/ppermute | solution.py:20
  9.3 0.0 collective-permute-start.2
  9.3 1.6 %collective-permute-done.3.refs_3_ = bf16[2,7168]{1,0:T(2,128)(2,1)S(1)} collective-permute-done((bf16[2,7168]{1,0:T(2,128)(2,1)S(1)}, bf16[2,7168]{1,0:T(2,128)(2,1)S(1)}, u32[]{:S(2)}, u32[]{:S(2)}) %collective-permute-start.3) | collective-permute-done | bytes 28704 | tf_op jit(solution)/shard_map/ppermute | solution.py:20
  11.0 0.0 collective-permute-start.1
  11.0 2.6 %collective-permute-done.2.refs_2_ = bf16[2,7168]{1,0:T(2,128)(2,1)S(1)} collective-permute-done((bf16[2,7168]{1,0:T(2,128)(2,1)S(1)}, bf16[2,7168]{1,0:T(2,128)(2,1)S(1)}, u32[]{:S(2)}, u32[]{:S(2)}) %collective-permute-start.2) | collective-permute-done | bytes 28704 | tf_op jit(solution)/shard_map/ppermute | solution.py:20
  13.6 0.7 %collective-permute-done.1.refs_1_ = bf16[2,7168]{1,0:T(2,128)(2,1)S(1)} collective-permute-done((bf16[2,7168]{1,0:T(2,128)(2,1)S(1)}, bf16[2,7168]{1,0:T(2,128)(2,1)S(1)}, u32[]{:S(2)}, u32[]{:S(2)}) %collective-permute-start.1) | collective-permute-done | bytes 28704 | tf_op jit(solution)/shard_map/ppermute | solution.py:20
  14.3 0.0 collective-permute-done.4.refs_10_
  14.3 0.0 collective-permute-done.5.refs_11_
  14.3 0.0 collective-permute-done.6.refs_12_
  14.3 1.0 %experts.1 = (f32[2,7168]{1,0:T(2,128)S(1)}, bf16[2,7168]{1,0:T(2,128)(2,1)S(1)}, bf16[2,7168]{1,0:T(2,128)(2,1)S(1)}, bf16[2,7168]{1,0:T(2,128)(2,1)S(1)}) custom-call(bf16[2,7168]{1,0:T(2,128)(2,1)S(1)} %pad_maximum_fusion.refs_0_, bf16[2,7168]{1,0:T(2,128)(2,1)S(1)} %collective-permute-done.1.refs_1_, bf16[2,7168]{1,0:T(2,128)(2,1)S(1)} %collective-permute-done.2.refs_2_, ...), custom_call_target="tpu_custom_call" | custom-call | tf_op jit(solution)/shard_map/experts/pallas_call | solution.py:125
  15.3 0.1 collective-permute-start.7
  15.4 3.7 %collective-permute-start.8 = (bf16[2,7168]{1,0:T(2,128)(2,1)S(1)}, bf16[2,7168]{1,0:T(2,128)(2,1)S(1)}, u32[]{:S(2)}, u32[]{:S(2)}) collective-permute-start(bf16[2,7168]{1,0:T(2,128)(2,1)S(1)} %get-tuple-element.37), channel_id=1, source_target_pairs={{0,12},{1,13},{2,14},{3,15},{4,8},{5,9},{6,10},{7,11},{8,4},{9,5},... | collective-permute-start | bytes 86024 | tf_op jit(solution)/shard_map/ppermute | solution.py:20
  19.1 0.1 collective-permute-start.9
  19.3 0.0 collective-permute-done.7
  19.3 1.6 %collective-permute-done.8 = bf16[2,7168]{1,0:T(2,128)(2,1)S(1)} collective-permute-done((bf16[2,7168]{1,0:T(2,128)(2,1)S(1)}, bf16[2,7168]{1,0:T(2,128)(2,1)S(1)}, u32[]{:S(2)}, u32[]{:S(2)}) %collective-permute-start.8) | collective-permute-done | bytes 28704 | tf_op jit(solution)/shard_map/ppermute | solution.py:20
  20.9 3.4 %collective-permute-done.9 = bf16[2,7168]{1,0:T(2,128)(2,1)S(1)} collective-permute-done((bf16[2,7168]{1,0:T(2,128)(2,1)S(1)}, bf16[2,7168]{1,0:T(2,128)(2,1)S(1)}, u32[]{:S(2)}, u32[]{:S(2)}) %collective-permute-start.9) | collective-permute-done | bytes 28704 | tf_op jit(solution)/shard_map/ppermute | solution.py:20
  24.2 0.1 convert_add_fusion
  24.3 1.6 %collective-permute-start.10 = (bf16[1,7168]{1,0:T(2,128)(2,1)S(1)}, bf16[1,7168]{1,0:T(2,128)(2,1)S(1)}, u32[]{:S(2)}, u32[]{:S(2)}) collective-permute-start(bf16[1,7168]{1,0:T(2,128)(2,1)S(1)} %slice.15), channel_id=1, source_target_pairs={{0,9},{1,8},{2,11},{3,10},{4,13},{5,12},{6,15},{7,14},{8,1},{9,0},... | collective-permute-start | bytes 43016 | tf_op jit(solution)/shard_map/ppermute | solution.py:20
  25.9 1.8 %collective-permute-done.10 = bf16[1,7168]{1,0:T(2,128)(2,1)S(1)} collective-permute-done((bf16[1,7168]{1,0:T(2,128)(2,1)S(1)}, bf16[1,7168]{1,0:T(2,128)(2,1)S(1)}, u32[]{:S(2)}, u32[]{:S(2)}) %collective-permute-start.10) | collective-permute-done | bytes 14368 | tf_op jit(solution)/shard_map/ppermute | solution.py:20
  27.7 0.7 %fusion = bf16[1,7168]{1,0:T(2,128)(2,1)} fusion(f32[2,7168]{1,0:T(2,128)S(1)} %convert_add_fusion, bf16[1,7168]{1,0:T(2,128)(2,1)S(1)} %collective-permute-done.10), kind=kLoop, calls=%fused_computation.3 | loop fusion | flops 21504 | bytes 57344 | tf_op jit(solution)/shard_map/convert_element_type | solution.py:144
  (1 shorter events, 0.0 us)
Async XLA Ops:
  0.0 5.4 %copy-start = (bf16[1,7168]{1,0:T(2,128)(2,1)S(1)}, bf16[1,7168]{1,0:T(2,128)(2,1)}, u32[]{:S(2)}) copy-start(bf16[1,7168]{1,0:T(2,128)(2,1)} %param.7) | copy-start | bytes 43012
  0.0 14.3 %collective-permute-start.4 = (bf16[3584,128]{1,0:T(8,128)(2,1)}, bf16[3584,128]{1,0:T(8,128)(2,1)S(1)}, u32[]{:S(2)}, u32[]{:S(2)}) collective-permute-start(bf16[3584,128]{1,0:T(8,128)(2,1)} %refs_0_.1), channel_id=1, source_target_pairs={{0,8},{8,0},{1,9},{9,1},{2,10},{10,2},{3,11},{11,3},{4,12},{12,4},... | collective-permute-start | bytes 2752520 | tf_op jit(solution)/shard_map/ppermute | solution.py:14
  0.5 13.9 %collective-permute-start.5 = (bf16[3584,128]{1,0:T(8,128)(2,1)}, bf16[3584,128]{1,0:T(8,128)(2,1)S(1)}, u32[]{:S(2)}, u32[]{:S(2)}) collective-permute-start(bf16[3584,128]{1,0:T(8,128)(2,1)} %refs_1_.1), channel_id=1, source_target_pairs={{0,8},{8,0},{1,9},{9,1},{2,10},{10,2},{3,11},{11,3},{4,12},{12,4},... | collective-permute-start | bytes 2752520 | tf_op jit(solution)/shard_map/ppermute | solution.py:14
  0.5 13.8 %collective-permute-start.6 = (bf16[128,3584]{1,0:T(8,128)(2,1)}, bf16[128,3584]{1,0:T(8,128)(2,1)S(1)}, u32[]{:S(2)}, u32[]{:S(2)}) collective-permute-start(bf16[128,3584]{1,0:T(8,128)(2,1)} %refs_2_.1), channel_id=1, source_target_pairs={{0,8},{8,0},{1,9},{9,1},{2,10},{10,2},{3,11},{11,3},{4,12},{12,4},... | collective-permute-start | bytes 2752520 | tf_op jit(solution)/shard_map/ppermute | solution.py:14
  1.0 4.4 %collective-permute-start = (bf16[1,7168]{1,0:T(2,128)(2,1)}, bf16[1,7168]{1,0:T(2,128)(2,1)S(1)}, u32[]{:S(2)}, u32[]{:S(2)}) collective-permute-start(bf16[1,7168]{1,0:T(2,128)(2,1)} %param.7), channel_id=1, source_target_pairs={{0,9},{1,8},{2,11},{3,10},{4,13},{5,12},{6,15},{7,14},{8,1},{9,0},... | collective-permute-start | bytes 43016 | tf_op jit(solution)/shard_map/ppermute | solution.py:20
  5.5 5.5 %collective-permute-start.3 = (bf16[2,7168]{1,0:T(2,128)(2,1)S(1)}, bf16[2,7168]{1,0:T(2,128)(2,1)S(1)}, u32[]{:S(2)}, u32[]{:S(2)}) collective-permute-start(bf16[2,7168]{1,0:T(2,128)(2,1)S(1)} %pad_maximum_fusion.refs_0_), channel_id=1, source_target_pairs={{0,14},{1,15},{2,12},{3,13},{4,10},{5,11},{6,8},{7,9},{8,6},{9,7},... | collective-permute-start | bytes 86024 | tf_op jit(solution)/shard_map/ppermute | solution.py:20
  9.3 4.3 %collective-permute-start.2 = (bf16[2,7168]{1,0:T(2,128)(2,1)S(1)}, bf16[2,7168]{1,0:T(2,128)(2,1)S(1)}, u32[]{:S(2)}, u32[]{:S(2)}) collective-permute-start(bf16[2,7168]{1,0:T(2,128)(2,1)S(1)} %pad_maximum_fusion.refs_0_), channel_id=1, source_target_pairs={{0,12},{1,13},{2,14},{3,15},{4,8},{5,9},{6,10},{7,11},{8,4},{9,5},... | collective-permute-start | bytes 86024 | tf_op jit(solution)/shard_map/ppermute | solution.py:20
  11.0 3.3 %collective-permute-start.1 = (bf16[2,7168]{1,0:T(2,128)(2,1)S(1)}, bf16[2,7168]{1,0:T(2,128)(2,1)S(1)}, u32[]{:S(2)}, u32[]{:S(2)}) collective-permute-start(bf16[2,7168]{1,0:T(2,128)(2,1)S(1)} %pad_maximum_fusion.refs_0_), channel_id=1, source_target_pairs={{0,10},{1,11},{2,8},{3,9},{4,14},{5,15},{6,12},{7,13},{8,2},{9,3},... | collective-permute-start | bytes 86024 | tf_op jit(solution)/shard_map/ppermute | solution.py:20
  15.3 3.9 %collective-permute-start.7 = (bf16[2,7168]{1,0:T(2,128)(2,1)S(1)}, bf16[2,7168]{1,0:T(2,128)(2,1)S(1)}, u32[]{:S(2)}, u32[]{:S(2)}) collective-permute-start(bf16[2,7168]{1,0:T(2,128)(2,1)S(1)} %get-tuple-element.36), channel_id=1, source_target_pairs={{0,10},{1,11},{2,8},{3,9},{4,14},{5,15},{6,12},{7,13},{8,2},{9,3},... | collective-permute-start | bytes 86024 | tf_op jit(solution)/shard_map/ppermute | solution.py:20
  15.4 5.5 %collective-permute-start.8 = (bf16[2,7168]{1,0:T(2,128)(2,1)S(1)}, bf16[2,7168]{1,0:T(2,128)(2,1)S(1)}, u32[]{:S(2)}, u32[]{:S(2)}) collective-permute-start(bf16[2,7168]{1,0:T(2,128)(2,1)S(1)} %get-tuple-element.37), channel_id=1, source_target_pairs={{0,12},{1,13},{2,14},{3,15},{4,8},{5,9},{6,10},{7,11},{8,4},{9,5},... | collective-permute-start | bytes 86024 | tf_op jit(solution)/shard_map/ppermute | solution.py:20
  19.1 5.1 %collective-permute-start.9 = (bf16[2,7168]{1,0:T(2,128)(2,1)S(1)}, bf16[2,7168]{1,0:T(2,128)(2,1)S(1)}, u32[]{:S(2)}, u32[]{:S(2)}) collective-permute-start(bf16[2,7168]{1,0:T(2,128)(2,1)S(1)} %get-tuple-element.38), channel_id=1, source_target_pairs={{0,14},{1,15},{2,12},{3,13},{4,10},{5,11},{6,8},{7,9},{8,6},{9,7},... | collective-permute-start | bytes 86024 | tf_op jit(solution)/shard_map/ppermute | solution.py:20
  24.3 3.4 %collective-permute-start.10 = (bf16[1,7168]{1,0:T(2,128)(2,1)S(1)}, bf16[1,7168]{1,0:T(2,128)(2,1)S(1)}, u32[]{:S(2)}, u32[]{:S(2)}) collective-permute-start(bf16[1,7168]{1,0:T(2,128)(2,1)S(1)} %slice.15), channel_id=1, source_target_pairs={{0,9},{1,8},{2,11},{3,10},{4,13},{5,12},{6,15},{7,14},{8,1},{9,0},... | collective-permute-start | bytes 43016 | tf_op jit(solution)/shard_map/ppermute | solution.py:20

commit v3 on v2

--- a/solution.py
+++ b/solution.py
@@ -114,12 +114,14 @@
         rows = jnp.concatenate(pieces, axis=0) if len(pieces) > 1 else pieces[0]
         if i == 1:
             here = stage(gate_weight, up_weight, down_weight, steering, block_rows, block_gates)
-            rows, here = lax.optimization_barrier((rows, here))
+            far = {n: swap_cores(w) for n, w in zip("gud", (gate_weight, up_weight, down_weight))}
+            rows, here, early = lax.optimization_barrier((rows, here, [far[n] for n in "g"]))
+            far.update(zip("g", early))
         pieces = [rows] + [exchange(rows, k * base, cross) for k in range(1, radix)]
         owners = [(o ^ (k * base), c ^ (cross if k else 0)) for k in range(radix) for o, c in owners]
     if here is None:
         here = stage(gate_weight, up_weight, down_weight, steering, block_rows, block_gates)
-    far = [swap_cores(w) for w in (gate_weight, up_weight, down_weight)]
+    far = [far[n] for n in "gud"]
     chunk = count // len(pieces)
     vmem = pl.BlockSpec(memory_space=pltpu.VMEM)
     outs = pl.pallas_call(
@@ -138,7 +140,7 @@
             chunk = total.shape[0] // radix
             sends = [total[k * chunk:(k + 1) * chunk].astype(jnp.bfloat16) for k in range(1, radix)]
             total = total[:chunk]
-        got = [exchange(s, k * base, cross) for k, s in enumerate(sends, 1)]
+        got = [exchange(s, k * base, cross) for k, s in reversed(list(enumerate(sends, 1)))]
         for g in got:
             total = total + g.astype(jnp.float32)
     return total.astype(jnp.bfloat16)

time: 28.5 us -> 25.4 us (0.89)
  waiting for transfers between devices: 11.7 us -> 8.71 us
    ppermute x8, waiting for transfers between devices: 11.7 us -> 8.7 us  [exchange(): return lax.ppermute(x, ('fsdp', 'ep'), pairs)]
  transfers between devices with their start and end apart: 11 -> 11, of which waited for: 6 -> 5; matrix products, arithmetic and copies ran while one was open for 0% -> 0% of each run, Pallas kernels for 6% -> 7%
where the time goes in v3:
time: 25.4 us; the launch traced here: 25.3 us
  starting transfers between devices  12.9 us (51%)
  waiting for transfers between devices  8.71 us (34%)
  Pallas kernels  2.79 us (11%)
  other arithmetic  0.78 us (3%)
    ppermute x8, starting transfers between devices, exchange(): return lax.ppermute(x, ('fsdp', 'ep'), pairs)  12 us
    ppermute x8, waiting for transfers between devices, exchange(): return lax.ppermute(x, ('fsdp', 'ep'), pairs)  8.7 us
    pallas_call x1, Pallas kernels, stage(): pl.pallas_call(stage_kernel, out_shape=[jax.ShapeDtypeStruct(a.shape, a.d...  1.79 us
    pallas_call x1, Pallas kernels, body(): pl.pallas_call(functools.partial(experts_kernel, owners, len(pieces)), ou...  1 us
    ppermute x3, starting transfers between devices, swap_cores(): return lax.ppermute(x, 'fsdp', [(0, 1), (1, 0)])  0.96 us
    convert_element_type x1, other arithmetic, body(): return total.astype(jnp.bfloat16)  0.65 us
  transfers between devices with their start and end apart: 11, of which 5 were waited for; matrix products, arithmetic and copies ran while one was open for 0% of the time, Pallas kernels for 7%

profile of v3, /device:TPU:0, one launch (start us, length us, event | category | flops | bytes accessed | tf_op | source)
XLA Modules:
  0.0 25.3 jit_solution(16826154628464653570)
XLA Ops:
  0.0 0.0 copy-start
  0.0 0.5 %collective-permute-start.1 = (bf16[3584,128]{1,0:T(8,128)(2,1)}, bf16[3584,128]{1,0:T(8,128)(2,1)S(1)}, u32[]{:S(2)}, u32[]{:S(2)}) collective-permute-start(bf16[3584,128]{1,0:T(8,128)(2,1)} %refs_0_.1), channel_id=1, source_target_pairs={{0,8},{8,0},{1,9},{9,1},{2,10},{10,2},{3,11},{11,3},{4,12},{12,4},... | collective-permute-start | bytes 2752520 | tf_op jit(solution)/shard_map/ppermute | solution.py:14
  0.5 0.1 collective-permute-start.5
  0.5 0.4 %collective-permute-start.6 = (bf16[128,3584]{1,0:T(8,128)(2,1)}, bf16[128,3584]{1,0:T(8,128)(2,1)S(1)}, u32[]{:S(2)}, u32[]{:S(2)}) collective-permute-start(bf16[128,3584]{1,0:T(8,128)(2,1)} %refs_2_.1), channel_id=1, source_target_pairs={{0,8},{8,0},{1,9},{9,1},{2,10},{10,2},{3,11},{11,3},{4,12},{12,4},... | collective-permute-start | bytes 2752520 | tf_op jit(solution)/shard_map/ppermute | solution.py:14
  1.0 2.6 %collective-permute-start = (bf16[1,7168]{1,0:T(2,128)(2,1)}, bf16[1,7168]{1,0:T(2,128)(2,1)S(1)}, u32[]{:S(2)}, u32[]{:S(2)}) collective-permute-start(bf16[1,7168]{1,0:T(2,128)(2,1)} %param.7), channel_id=1, source_target_pairs={{0,9},{1,8},{2,11},{3,10},{4,13},{5,12},{6,15},{7,14},{8,1},{9,0},... | collective-permute-start | bytes 43016 | tf_op jit(solution)/shard_map/ppermute | solution.py:20
  3.6 1.8 %stage.1 = (bf16[3584,128]{1,0:T(8,128)(2,1)S(1)}, bf16[3584,128]{1,0:T(8,128)(2,1)S(1)}, bf16[128,3584]{1,0:T(8,128)(2,1)S(1)}, bf16[1,7168]{1,0:T(2,128)(2,1)S...) custom-call(bf16[3584,128]{1,0:T(8,128)(2,1)} %refs_0_.1, bf16[3584,128]{1,0:T(8,128)(2,1)} %refs_1_.1, ...), custom_call_target="tpu_custom_call" | custom-call | tf_op jit(solution)/shard_map/stage/pallas_call | solution.py:47
  5.4 0.0 collective-permute-done
  5.4 0.0 copy-done
  5.4 0.1 pad_maximum_fusion.refs_0_
  5.5 0.0 collective-permute-done.1.refs_10_
  5.5 3.9 %collective-permute-start.4 = (bf16[2,7168]{1,0:T(2,128)(2,1)S(1)}, bf16[2,7168]{1,0:T(2,128)(2,1)S(1)}, u32[]{:S(2)}, u32[]{:S(2)}) collective-permute-start(bf16[2,7168]{1,0:T(2,128)(2,1)S(1)} %pad_maximum_fusion.refs_0_), channel_id=1, source_target_pairs={{0,14},{1,15},{2,12},{3,13},{4,10},{5,11},{6,8},{7,9},{8,6},{9,7},... | collective-permute-start | bytes 86024 | tf_op jit(solution)/shard_map/ppermute | solution.py:20
  9.3 0.0 collective-permute-start.3
  9.3 0.3 %collective-permute-start.2 = (bf16[2,7168]{1,0:T(2,128)(2,1)S(1)}, bf16[2,7168]{1,0:T(2,128)(2,1)S(1)}, u32[]{:S(2)}, u32[]{:S(2)}) collective-permute-start(bf16[2,7168]{1,0:T(2,128)(2,1)S(1)} %pad_maximum_fusion.refs_0_), channel_id=1, source_target_pairs={{0,10},{1,11},{2,8},{3,9},{4,14},{5,15},{6,12},{7,13},{8,2},{9,3},... | collective-permute-start | bytes 86024 | tf_op jit(solution)/shard_map/ppermute | solution.py:20
  9.7 0.0 collective-permute-done.5.refs_11_
  9.7 0.0 collective-permute-done.6.refs_12_
  9.7 1.3 %collective-permute-done.4.refs_3_ = bf16[2,7168]{1,0:T(2,128)(2,1)S(1)} collective-permute-done((bf16[2,7168]{1,0:T(2,128)(2,1)S(1)}, bf16[2,7168]{1,0:T(2,128)(2,1)S(1)}, u32[]{:S(2)}, u32[]{:S(2)}) %collective-permute-start.4) | collective-permute-done | bytes 28704 | tf_op jit(solution)/shard_map/ppermute | solution.py:20
  11.0 2.6 %collective-permute-done.3.refs_2_ = bf16[2,7168]{1,0:T(2,128)(2,1)S(1)} collective-permute-done((bf16[2,7168]{1,0:T(2,128)(2,1)S(1)}, bf16[2,7168]{1,0:T(2,128)(2,1)S(1)}, u32[]{:S(2)}, u32[]{:S(2)}) %collective-permute-start.3) | collective-permute-done | bytes 28704 | tf_op jit(solution)/shard_map/ppermute | solution.py:20
  13.6 0.0 collective-permute-done.2.refs_1_
  13.6 1.0 %experts.1 = (f32[2,7168]{1,0:T(2,128)S(1)}, bf16[2,7168]{1,0:T(2,128)(2,1)S(1)}, bf16[2,7168]{1,0:T(2,128)(2,1)S(1)}, bf16[2,7168]{1,0:T(2,128)(2,1)S(1)}) custom-call(bf16[2,7168]{1,0:T(2,128)(2,1)S(1)} %pad_maximum_fusion.refs_0_, bf16[2,7168]{1,0:T(2,128)(2,1)S(1)} %collective-permute-done.2.refs_1_, bf16[2,7168]{1,0:T(2,128)(2,1)S(1)} %collective-permute-done.3.refs_2_, ...), custom_call_target="tpu_custom_call" | custom-call | tf_op jit(solution)/shard_map/experts/pallas_call | solution.py:127
  14.6 1.6 %collective-permute-start.7 = (bf16[2,7168]{1,0:T(2,128)(2,1)S(1)}, bf16[2,7168]{1,0:T(2,128)(2,1)S(1)}, u32[]{:S(2)}, u32[]{:S(2)}) collective-permute-start(bf16[2,7168]{1,0:T(2,128)(2,1)S(1)} %get-tuple-element.38), channel_id=1, source_target_pairs={{0,14},{1,15},{2,12},{3,13},{4,10},{5,11},{6,8},{7,9},{8,6},{9,7},... | collective-permute-start | bytes 86024 | tf_op jit(solution)/shard_map/ppermute | solution.py:20
  16.2 0.2 collective-permute-start.8
  16.4 2.1 %collective-permute-start.9 = (bf16[2,7168]{1,0:T(2,128)(2,1)S(1)}, bf16[2,7168]{1,0:T(2,128)(2,1)S(1)}, u32[]{:S(2)}, u32[]{:S(2)}) collective-permute-start(bf16[2,7168]{1,0:T(2,128)(2,1)S(1)} %get-tuple-element.40), channel_id=1, source_target_pairs={{0,10},{1,11},{2,8},{3,9},{4,14},{5,15},{6,12},{7,13},{8,2},{9,3},... | collective-permute-start | bytes 86024 | tf_op jit(solution)/shard_map/ppermute | solution.py:20
  18.5 1.2 %collective-permute-done.7 = bf16[2,7168]{1,0:T(2,128)(2,1)S(1)} collective-permute-done((bf16[2,7168]{1,0:T(2,128)(2,1)S(1)}, bf16[2,7168]{1,0:T(2,128)(2,1)S(1)}, u32[]{:S(2)}, u32[]{:S(2)}) %collective-permute-start.7) | collective-permute-done | bytes 28704 | tf_op jit(solution)/shard_map/ppermute | solution.py:20
  19.8 1.4 %collective-permute-done.8 = bf16[2,7168]{1,0:T(2,128)(2,1)S(1)} collective-permute-done((bf16[2,7168]{1,0:T(2,128)(2,1)S(1)}, bf16[2,7168]{1,0:T(2,128)(2,1)S(1)}, u32[]{:S(2)}, u32[]{:S(2)}) %collective-permute-start.8) | collective-permute-done | bytes 28704 | tf_op jit(solution)/shard_map/ppermute | solution.py:20
  21.2 0.0 collective-permute-done.9
  21.2 0.1 convert_add_fusion
  21.3 1.3 %collective-permute-start.10 = (bf16[1,7168]{1,0:T(2,128)(2,1)S(1)}, bf16[1,7168]{1,0:T(2,128)(2,1)S(1)}, u32[]{:S(2)}, u32[]{:S(2)}) collective-permute-start(bf16[1,7168]{1,0:T(2,128)(2,1)S(1)} %slice.15), channel_id=1, source_target_pairs={{0,9},{1,8},{2,11},{3,10},{4,13},{5,12},{6,15},{7,14},{8,1},{9,0},... | collective-permute-start | bytes 43016 | tf_op jit(solution)/shard_map/ppermute | solution.py:20
  22.5 2.1 %collective-permute-done.10 = bf16[1,7168]{1,0:T(2,128)(2,1)S(1)} collective-permute-done((bf16[1,7168]{1,0:T(2,128)(2,1)S(1)}, bf16[1,7168]{1,0:T(2,128)(2,1)S(1)}, u32[]{:S(2)}, u32[]{:S(2)}) %collective-permute-start.10) | collective-permute-done | bytes 14368 | tf_op jit(solution)/shard_map/ppermute | solution.py:20
  24.6 0.7 %fusion = bf16[1,7168]{1,0:T(2,128)(2,1)} fusion(f32[2,7168]{1,0:T(2,128)S(1)} %convert_add_fusion, bf16[1,7168]{1,0:T(2,128)(2,1)S(1)} %collective-permute-done.10), kind=kLoop, calls=%fused_computation.3 | loop fusion | flops 21504 | bytes 57344 | tf_op jit(solution)/shard_map/convert_element_type | solution.py:146
  (1 shorter events, 0.0 us)
Async XLA Ops:
  0.0 5.4 %copy-start = (bf16[1,7168]{1,0:T(2,128)(2,1)S(1)}, bf16[1,7168]{1,0:T(2,128)(2,1)}, u32[]{:S(2)}) copy-start(bf16[1,7168]{1,0:T(2,128)(2,1)} %param.7) | copy-start | bytes 43012
  0.0 5.5 %collective-permute-start.1 = (bf16[3584,128]{1,0:T(8,128)(2,1)}, bf16[3584,128]{1,0:T(8,128)(2,1)S(1)}, u32[]{:S(2)}, u32[]{:S(2)}) collective-permute-start(bf16[3584,128]{1,0:T(8,128)(2,1)} %refs_0_.1), channel_id=1, source_target_pairs={{0,8},{8,0},{1,9},{9,1},{2,10},{10,2},{3,11},{11,3},{4,12},{12,4},... | collective-permute-start | bytes 2752520 | tf_op jit(solution)/shard_map/ppermute | solution.py:14
  0.5 9.2 %collective-permute-start.5 = (bf16[3584,128]{1,0:T(8,128)(2,1)}, bf16[3584,128]{1,0:T(8,128)(2,1)S(1)}, u32[]{:S(2)}, u32[]{:S(2)}) collective-permute-start(bf16[3584,128]{1,0:T(8,128)(2,1)} %refs_1_.1), channel_id=1, source_target_pairs={{0,8},{8,0},{1,9},{9,1},{2,10},{10,2},{3,11},{11,3},{4,12},{12,4},... | collective-permute-start | bytes 2752520 | tf_op jit(solution)/shard_map/ppermute | solution.py:14
  0.5 9.1 %collective-permute-start.6 = (bf16[128,3584]{1,0:T(8,128)(2,1)}, bf16[128,3584]{1,0:T(8,128)(2,1)S(1)}, u32[]{:S(2)}, u32[]{:S(2)}) collective-permute-start(bf16[128,3584]{1,0:T(8,128)(2,1)} %refs_2_.1), channel_id=1, source_target_pairs={{0,8},{8,0},{1,9},{9,1},{2,10},{10,2},{3,11},{11,3},{4,12},{12,4},... | collective-permute-start | bytes 2752520 | tf_op jit(solution)/shard_map/ppermute | solution.py:14
  1.0 4.4 %collective-permute-start = (bf16[1,7168]{1,0:T(2,128)(2,1)}, bf16[1,7168]{1,0:T(2,128)(2,1)S(1)}, u32[]{:S(2)}, u32[]{:S(2)}) collective-permute-start(bf16[1,7168]{1,0:T(2,128)(2,1)} %param.7), channel_id=1, source_target_pairs={{0,9},{1,8},{2,11},{3,10},{4,13},{5,12},{6,15},{7,14},{8,1},{9,0},... | collective-permute-start | bytes 43016 | tf_op jit(solution)/shard_map/ppermute | solution.py:20
  5.5 5.5 %collective-permute-start.4 = (bf16[2,7168]{1,0:T(2,128)(2,1)S(1)}, bf16[2,7168]{1,0:T(2,128)(2,1)S(1)}, u32[]{:S(2)}, u32[]{:S(2)}) collective-permute-start(bf16[2,7168]{1,0:T(2,128)(2,1)S(1)} %pad_maximum_fusion.refs_0_), channel_id=1, source_target_pairs={{0,14},{1,15},{2,12},{3,13},{4,10},{5,11},{6,8},{7,9},{8,6},{9,7},... | collective-permute-start | bytes 86024 | tf_op jit(solution)/shard_map/ppermute | solution.py:20
  9.3 4.3 %collective-permute-start.3 = (bf16[2,7168]{1,0:T(2,128)(2,1)S(1)}, bf16[2,7168]{1,0:T(2,128)(2,1)S(1)}, u32[]{:S(2)}, u32[]{:S(2)}) collective-permute-start(bf16[2,7168]{1,0:T(2,128)(2,1)S(1)} %pad_maximum_fusion.refs_0_), channel_id=1, source_target_pairs={{0,12},{1,13},{2,14},{3,15},{4,8},{5,9},{6,10},{7,11},{8,4},{9,5},... | collective-permute-start | bytes 86024 | tf_op jit(solution)/shard_map/ppermute | solution.py:20
  9.3 4.3 %collective-permute-start.2 = (bf16[2,7168]{1,0:T(2,128)(2,1)S(1)}, bf16[2,7168]{1,0:T(2,128)(2,1)S(1)}, u32[]{:S(2)}, u32[]{:S(2)}) collective-permute-start(bf16[2,7168]{1,0:T(2,128)(2,1)S(1)} %pad_maximum_fusion.refs_0_), channel_id=1, source_target_pairs={{0,10},{1,11},{2,8},{3,9},{4,14},{5,15},{6,12},{7,13},{8,2},{9,3},... | collective-permute-start | bytes 86024 | tf_op jit(solution)/shard_map/ppermute | solution.py:20
  14.6 5.2 %collective-permute-start.7 = (bf16[2,7168]{1,0:T(2,128)(2,1)S(1)}, bf16[2,7168]{1,0:T(2,128)(2,1)S(1)}, u32[]{:S(2)}, u32[]{:S(2)}) collective-permute-start(bf16[2,7168]{1,0:T(2,128)(2,1)S(1)} %get-tuple-element.38), channel_id=1, source_target_pairs={{0,14},{1,15},{2,12},{3,13},{4,10},{5,11},{6,8},{7,9},{8,6},{9,7},... | collective-permute-start | bytes 86024 | tf_op jit(solution)/shard_map/ppermute | solution.py:20
  16.2 4.9 %collective-permute-start.8 = (bf16[2,7168]{1,0:T(2,128)(2,1)S(1)}, bf16[2,7168]{1,0:T(2,128)(2,1)S(1)}, u32[]{:S(2)}, u32[]{:S(2)}) collective-permute-start(bf16[2,7168]{1,0:T(2,128)(2,1)S(1)} %get-tuple-element.39), channel_id=1, source_target_pairs={{0,12},{1,13},{2,14},{3,15},{4,8},{5,9},{6,10},{7,11},{8,4},{9,5},... | collective-permute-start | bytes 86024 | tf_op jit(solution)/shard_map/ppermute | solution.py:20
  16.4 4.7 %collective-permute-start.9 = (bf16[2,7168]{1,0:T(2,128)(2,1)S(1)}, bf16[2,7168]{1,0:T(2,128)(2,1)S(1)}, u32[]{:S(2)}, u32[]{:S(2)}) collective-permute-start(bf16[2,7168]{1,0:T(2,128)(2,1)S(1)} %get-tuple-element.40), channel_id=1, source_target_pairs={{0,10},{1,11},{2,8},{3,9},{4,14},{5,15},{6,12},{7,13},{8,2},{9,3},... | collective-permute-start | bytes 86024 | tf_op jit(solution)/shard_map/ppermute | solution.py:20
  21.3 3.4 %collective-permute-start.10 = (bf16[1,7168]{1,0:T(2,128)(2,1)S(1)}, bf16[1,7168]{1,0:T(2,128)(2,1)S(1)}, u32[]{:S(2)}, u32[]{:S(2)}) collective-permute-start(bf16[1,7168]{1,0:T(2,128)(2,1)S(1)} %slice.15), channel_id=1, source_target_pairs={{0,9},{1,8},{2,11},{3,10},{4,13},{5,12},{6,15},{7,14},{8,1},{9,0},... | collective-permute-start | bytes 43016 | tf_op jit(solution)/shard_map/ppermute | solution.py:20

commit v4 on v3

--- a/solution.py
+++ b/solution.py
@@ -21,13 +21,15 @@
 
 
 def stages(count):
-    steps = [(1, 2, 1)] if count > 1 else []
+    if count == 8:
+        return [[(4, 1)], [(1, 1), (2, 1), (3, 1)]]
+    plan = [[(1, 1)]] if count > 1 else []
     base = 2
     while base < count:
         radix = 4 if base * 4 <= count else 2
-        steps.append((base, radix, 1))
+        plan.append([(k * base, 1) for k in range(1, radix)])
         base *= radix
-    return steps
+    return plan
 
 
 def dot(a, b):
@@ -110,15 +112,15 @@
     pieces = [tokens]
     owners = [(0, 0)]
     steps = stages(count)
-    for i, (base, radix, cross) in enumerate(steps):
+    for i, hops in enumerate(steps):
         rows = jnp.concatenate(pieces, axis=0) if len(pieces) > 1 else pieces[0]
         if i == 1:
             here = stage(gate_weight, up_weight, down_weight, steering, block_rows, block_gates)
             far = {n: swap_cores(w) for n, w in zip("gud", (gate_weight, up_weight, down_weight))}
             rows, here, early = lax.optimization_barrier((rows, here, [far[n] for n in "g"]))
             far.update(zip("g", early))
-        pieces = [rows] + [exchange(rows, k * base, cross) for k in range(1, radix)]
-        owners = [(o ^ (k * base), c ^ (cross if k else 0)) for k in range(radix) for o, c in owners]
+        pieces = [rows] + [exchange(rows, d, c) for d, c in hops]
+        owners = owners + [(o ^ d, c ^ x) for d, x in hops for o, c in owners]
     if here is None:
         here = stage(gate_weight, up_weight, down_weight, steering, block_rows, block_gates)
     far = [far[n] for n in "gud"]
@@ -135,12 +137,12 @@
         name="experts",
     )(*pieces, *here, *far)
     total, sends = outs[0], list(outs[1:])
-    for i, (base, radix, cross) in enumerate(reversed(steps)):
+    for i, hops in enumerate(reversed(steps)):
         if i:
-            chunk = total.shape[0] // radix
-            sends = [total[k * chunk:(k + 1) * chunk].astype(jnp.bfloat16) for k in range(1, radix)]
+            chunk = total.shape[0] // (len(hops) + 1)
+            sends = [total[(k + 1) * chunk:(k + 2) * chunk].astype(jnp.bfloat16) for k in range(len(hops))]
             total = total[:chunk]
-        got = [exchange(s, k * base, cross) for k, s in reversed(list(enumerate(sends, 1)))]
+        got = [exchange(s, d, c) for s, (d, c) in reversed(list(zip(sends, hops)))]
         for g in got:
             total = total + g.astype(jnp.float32)
     return total.astype(jnp.bfloat16)

time: 25.4 us -> 24 us (0.945)
  waiting for transfers between devices: 8.71 us -> 6.76 us
  starting transfers between devices: 12.9 us -> 13.4 us
    ppermute x8, waiting for transfers between devices: 8.7 us -> 6.75 us  [exchange(): return lax.ppermute(x, ('fsdp', 'ep'), pairs)]
    ppermute x8, starting transfers between devices: 12 us -> 12.5 us  [exchange(): return lax.ppermute(x, ('fsdp', 'ep'), pairs)]
  transfers between devices with their start and end apart: 11 -> 11, of which waited for: 5 -> 7; matrix products, arithmetic and copies ran while one was open for 0% -> 0% of each run, Pallas kernels for 7% -> 8%
where the time goes in v4:
time: 24 us; the launch traced here: 23.8 us
  starting transfers between devices  13.4 us (56%)
  waiting for transfers between devices  6.76 us (28%)
  Pallas kernels  2.79 us (12%)
  other arithmetic  0.78 us (3%)
    ppermute x8, starting transfers between devices, exchange(): return lax.ppermute(x, ('fsdp', 'ep'), pairs)  12.5 us
    ppermute x8, waiting for transfers between devices, exchange(): return lax.ppermute(x, ('fsdp', 'ep'), pairs)  6.75 us
    pallas_call x1, Pallas kernels, stage(): pl.pallas_call(stage_kernel, out_shape=[jax.ShapeDtypeStruct(a.shape, a.d...  1.79 us
    pallas_call x1, Pallas kernels, body(): pl.pallas_call(functools.partial(experts_kernel, owners, len(pieces)), ou...  1 us
    ppermute x3, starting transfers between devices, swap_cores(): return lax.ppermute(x, 'fsdp', [(0, 1), (1, 0)])  0.96 us
    convert_element_type x1, other arithmetic, body(): return total.astype(jnp.bfloat16)  0.65 us
  transfers between devices with their start and end apart: 11, of which 7 were waited for; matrix products, arithmetic and copies ran while one was open for 0% of the time, Pallas kernels for 8%

profile of v4, /device:TPU:0, one launch (start us, length us, event | category | flops | bytes accessed | tf_op | source)
XLA Modules:
  0.0 23.8 jit_solution(3229734805289972148)
XLA Ops:
  0.0 0.0 copy-start
  0.0 0.5 %collective-permute-start.1 = (bf16[3584,128]{1,0:T(8,128)(2,1)}, bf16[3584,128]{1,0:T(8,128)(2,1)S(1)}, u32[]{:S(2)}, u32[]{:S(2)}) collective-permute-start(bf16[3584,128]{1,0:T(8,128)(2,1)} %refs_0_.1), channel_id=1, source_target_pairs={{0,8},{8,0},{1,9},{9,1},{2,10},{10,2},{3,11},{11,3},{4,12},{12,4},... | collective-permute-start | bytes 2752520 | tf_op jit(solution)/shard_map/ppermute | solution.py:14
  0.5 0.1 collective-permute-start.5
  0.5 0.4 %collective-permute-start.6 = (bf16[128,3584]{1,0:T(8,128)(2,1)}, bf16[128,3584]{1,0:T(8,128)(2,1)S(1)}, u32[]{:S(2)}, u32[]{:S(2)}) collective-permute-start(bf16[128,3584]{1,0:T(8,128)(2,1)} %refs_2_.1), channel_id=1, source_target_pairs={{0,8},{8,0},{1,9},{9,1},{2,10},{10,2},{3,11},{11,3},{4,12},{12,4},... | collective-permute-start | bytes 2752520 | tf_op jit(solution)/shard_map/ppermute | solution.py:14
  1.0 3.7 %collective-permute-start = (bf16[1,7168]{1,0:T(2,128)(2,1)}, bf16[1,7168]{1,0:T(2,128)(2,1)S(1)}, u32[]{:S(2)}, u32[]{:S(2)}) collective-permute-start(bf16[1,7168]{1,0:T(2,128)(2,1)} %param.7), channel_id=1, source_target_pairs={{0,12},{1,13},{2,14},{3,15},{4,8},{5,9},{6,10},{7,11},{8,4},{9,5},... | collective-permute-start | bytes 43016 | tf_op jit(solution)/shard_map/ppermute | solution.py:20
  4.7 1.8 %stage.1 = (bf16[3584,128]{1,0:T(8,128)(2,1)S(1)}, bf16[3584,128]{1,0:T(8,128)(2,1)S(1)}, bf16[128,3584]{1,0:T(8,128)(2,1)S(1)}, bf16[1,7168]{1,0:T(2,128)(2,1)S...) custom-call(bf16[3584,128]{1,0:T(8,128)(2,1)} %refs_0_.1, bf16[3584,128]{1,0:T(8,128)(2,1)} %refs_1_.1, ...), custom_call_target="tpu_custom_call" | custom-call | tf_op jit(solution)/shard_map/stage/pallas_call | solution.py:49
  6.5 0.0 collective-permute-done
  6.5 0.0 copy-done
  6.5 0.1 pad_maximum_fusion.refs_0_
  6.6 0.0 collective-permute-done.1.refs_10_
  6.6 2.6 %collective-permute-start.4 = (bf16[2,7168]{1,0:T(2,128)(2,1)S(1)}, bf16[2,7168]{1,0:T(2,128)(2,1)S(1)}, u32[]{:S(2)}, u32[]{:S(2)}) collective-permute-start(bf16[2,7168]{1,0:T(2,128)(2,1)S(1)} %pad_maximum_fusion.refs_0_), channel_id=1, source_target_pairs={{0,11},{1,10},{2,9},{3,8},{4,15},{5,14},{6,13},{7,12},{8,3},{9,2},... | collective-permute-start | bytes 86024 | tf_op jit(solution)/shard_map/ppermute | solution.py:20
  9.1 0.2 collective-permute-start.3
  9.3 0.2 collective-permute-start.2
  9.6 0.0 collective-permute-done.5.refs_11_
  9.6 0.0 collective-permute-done.6.refs_12_
  9.6 1.3 %collective-permute-done.4.refs_3_ = bf16[2,7168]{1,0:T(2,128)(2,1)S(1)} collective-permute-done((bf16[2,7168]{1,0:T(2,128)(2,1)S(1)}, bf16[2,7168]{1,0:T(2,128)(2,1)S(1)}, u32[]{:S(2)}, u32[]{:S(2)}) %collective-permute-start.4) | collective-permute-done | bytes 28704 | tf_op jit(solution)/shard_map/ppermute | solution.py:20
  10.8 1.6 %collective-permute-done.3.refs_2_ = bf16[2,7168]{1,0:T(2,128)(2,1)S(1)} collective-permute-done((bf16[2,7168]{1,0:T(2,128)(2,1)S(1)}, bf16[2,7168]{1,0:T(2,128)(2,1)S(1)}, u32[]{:S(2)}, u32[]{:S(2)}) %collective-permute-start.3) | collective-permute-done | bytes 28704 | tf_op jit(solution)/shard_map/ppermute | solution.py:20
  12.4 0.2 collective-permute-done.2.refs_1_
  12.7 1.0 %experts.1 = (f32[2,7168]{1,0:T(2,128)S(1)}, bf16[2,7168]{1,0:T(2,128)(2,1)S(1)}, bf16[2,7168]{1,0:T(2,128)(2,1)S(1)}, bf16[2,7168]{1,0:T(2,128)(2,1)S(1)}) custom-call(bf16[2,7168]{1,0:T(2,128)(2,1)S(1)} %pad_maximum_fusion.refs_0_, bf16[2,7168]{1,0:T(2,128)(2,1)S(1)} %collective-permute-done.2.refs_1_, bf16[2,7168]{1,0:T(2,128)(2,1)S(1)} %collective-permute-done.3.refs_2_, ...), custom_call_target="tpu_custom_call" | custom-call | tf_op jit(solution)/shard_map/experts/pallas_call | solution.py:129
  13.7 1.6 %collective-permute-start.7 = (bf16[2,7168]{1,0:T(2,128)(2,1)S(1)}, bf16[2,7168]{1,0:T(2,128)(2,1)S(1)}, u32[]{:S(2)}, u32[]{:S(2)}) collective-permute-start(bf16[2,7168]{1,0:T(2,128)(2,1)S(1)} %get-tuple-element.38), channel_id=1, source_target_pairs={{0,11},{1,10},{2,9},{3,8},{4,15},{5,14},{6,13},{7,12},{8,3},{9,2},... | collective-permute-start | bytes 86024 | tf_op jit(solution)/shard_map/ppermute | solution.py:20
  15.2 0.3 %collective-permute-start.8 = (bf16[2,7168]{1,0:T(2,128)(2,1)S(1)}, bf16[2,7168]{1,0:T(2,128)(2,1)S(1)}, u32[]{:S(2)}, u32[]{:S(2)}) collective-permute-start(bf16[2,7168]{1,0:T(2,128)(2,1)S(1)} %get-tuple-element.39), channel_id=1, source_target_pairs={{0,10},{1,11},{2,8},{3,9},{4,14},{5,15},{6,12},{7,13},{8,2},{9,3},... | collective-permute-start | bytes 86024 | tf_op jit(solution)/shard_map/ppermute | solution.py:20
  15.5 1.4 %collective-permute-start.9 = (bf16[2,7168]{1,0:T(2,128)(2,1)S(1)}, bf16[2,7168]{1,0:T(2,128)(2,1)S(1)}, u32[]{:S(2)}, u32[]{:S(2)}) collective-permute-start(bf16[2,7168]{1,0:T(2,128)(2,1)S(1)} %get-tuple-element.40), channel_id=1, source_target_pairs={{0,9},{1,8},{2,11},{3,10},{4,13},{5,12},{6,15},{7,14},{8,1},{9,0},... | collective-permute-start | bytes 86024 | tf_op jit(solution)/shard_map/ppermute | solution.py:20
  16.9 1.0 %collective-permute-done.7 = bf16[2,7168]{1,0:T(2,128)(2,1)S(1)} collective-permute-done((bf16[2,7168]{1,0:T(2,128)(2,1)S(1)}, bf16[2,7168]{1,0:T(2,128)(2,1)S(1)}, u32[]{:S(2)}, u32[]{:S(2)}) %collective-permute-start.7) | collective-permute-done | bytes 28704 | tf_op jit(solution)/shard_map/ppermute | solution.py:20
  17.9 0.6 %collective-permute-done.8 = bf16[2,7168]{1,0:T(2,128)(2,1)S(1)} collective-permute-done((bf16[2,7168]{1,0:T(2,128)(2,1)S(1)}, bf16[2,7168]{1,0:T(2,128)(2,1)S(1)}, u32[]{:S(2)}, u32[]{:S(2)}) %collective-permute-start.8) | collective-permute-done | bytes 28704 | tf_op jit(solution)/shard_map/ppermute | solution.py:20
  18.5 0.3 %collective-permute-done.9 = bf16[2,7168]{1,0:T(2,128)(2,1)S(1)} collective-permute-done((bf16[2,7168]{1,0:T(2,128)(2,1)S(1)}, bf16[2,7168]{1,0:T(2,128)(2,1)S(1)}, u32[]{:S(2)}, u32[]{:S(2)}) %collective-permute-start.9) | collective-permute-done | bytes 28704 | tf_op jit(solution)/shard_map/ppermute | solution.py:20
  18.8 0.1 convert_add_fusion
  18.9 2.5 %collective-permute-start.10 = (bf16[1,7168]{1,0:T(2,128)(2,1)S(1)}, bf16[1,7168]{1,0:T(2,128)(2,1)S(1)}, u32[]{:S(2)}, u32[]{:S(2)}) collective-permute-start(bf16[1,7168]{1,0:T(2,128)(2,1)S(1)} %slice.15), channel_id=1, source_target_pairs={{0,12},{1,13},{2,14},{3,15},{4,8},{5,9},{6,10},{7,11},{8,4},{9,5},... | collective-permute-start | bytes 43016 | tf_op jit(solution)/shard_map/ppermute | solution.py:20
  21.5 1.7 %collective-permute-done.10 = bf16[1,7168]{1,0:T(2,128)(2,1)S(1)} collective-permute-done((bf16[1,7168]{1,0:T(2,128)(2,1)S(1)}, bf16[1,7168]{1,0:T(2,128)(2,1)S(1)}, u32[]{:S(2)}, u32[]{:S(2)}) %collective-permute-start.10) | collective-permute-done | bytes 14368 | tf_op jit(solution)/shard_map/ppermute | solution.py:20
  23.2 0.7 %fusion = bf16[1,7168]{1,0:T(2,128)(2,1)} fusion(f32[2,7168]{1,0:T(2,128)S(1)} %convert_add_fusion, bf16[1,7168]{1,0:T(2,128)(2,1)S(1)} %collective-permute-done.10), kind=kLoop, calls=%fused_computation.3 | loop fusion | flops 21504 | bytes 57344 | tf_op jit(solution)/shard_map/convert_element_type | solution.py:148
  (1 shorter events, 0.0 us)
Async XLA Ops:
  0.0 6.5 %copy-start = (bf16[1,7168]{1,0:T(2,128)(2,1)S(1)}, bf16[1,7168]{1,0:T(2,128)(2,1)}, u32[]{:S(2)}) copy-start(bf16[1,7168]{1,0:T(2,128)(2,1)} %param.7) | copy-start | bytes 43012
  0.0 6.6 %collective-permute-start.1 = (bf16[3584,128]{1,0:T(8,128)(2,1)}, bf16[3584,128]{1,0:T(8,128)(2,1)S(1)}, u32[]{:S(2)}, u32[]{:S(2)}) collective-permute-start(bf16[3584,128]{1,0:T(8,128)(2,1)} %refs_0_.1), channel_id=1, source_target_pairs={{0,8},{8,0},{1,9},{9,1},{2,10},{10,2},{3,11},{11,3},{4,12},{12,4},... | collective-permute-start | bytes 2752520 | tf_op jit(solution)/shard_map/ppermute | solution.py:14
  0.5 9.1 %collective-permute-start.5 = (bf16[3584,128]{1,0:T(8,128)(2,1)}, bf16[3584,128]{1,0:T(8,128)(2,1)S(1)}, u32[]{:S(2)}, u32[]{:S(2)}) collective-permute-start(bf16[3584,128]{1,0:T(8,128)(2,1)} %refs_1_.1), channel_id=1, source_target_pairs={{0,8},{8,0},{1,9},{9,1},{2,10},{10,2},{3,11},{11,3},{4,12},{12,4},... | collective-permute-start | bytes 2752520 | tf_op jit(solution)/shard_map/ppermute | solution.py:14
  0.5 9.1 %collective-permute-start.6 = (bf16[128,3584]{1,0:T(8,128)(2,1)}, bf16[128,3584]{1,0:T(8,128)(2,1)S(1)}, u32[]{:S(2)}, u32[]{:S(2)}) collective-permute-start(bf16[128,3584]{1,0:T(8,128)(2,1)} %refs_2_.1), channel_id=1, source_target_pairs={{0,8},{8,0},{1,9},{9,1},{2,10},{10,2},{3,11},{11,3},{4,12},{12,4},... | collective-permute-start | bytes 2752520 | tf_op jit(solution)/shard_map/ppermute | solution.py:14
  1.0 5.5 %collective-permute-start = (bf16[1,7168]{1,0:T(2,128)(2,1)}, bf16[1,7168]{1,0:T(2,128)(2,1)S(1)}, u32[]{:S(2)}, u32[]{:S(2)}) collective-permute-start(bf16[1,7168]{1,0:T(2,128)(2,1)} %param.7), channel_id=1, source_target_pairs={{0,12},{1,13},{2,14},{3,15},{4,8},{5,9},{6,10},{7,11},{8,4},{9,5},... | collective-permute-start | bytes 43016 | tf_op jit(solution)/shard_map/ppermute | solution.py:20
  6.6 4.3 %collective-permute-start.4 = (bf16[2,7168]{1,0:T(2,128)(2,1)S(1)}, bf16[2,7168]{1,0:T(2,128)(2,1)S(1)}, u32[]{:S(2)}, u32[]{:S(2)}) collective-permute-start(bf16[2,7168]{1,0:T(2,128)(2,1)S(1)} %pad_maximum_fusion.refs_0_), channel_id=1, source_target_pairs={{0,11},{1,10},{2,9},{3,8},{4,15},{5,14},{6,13},{7,12},{8,3},{9,2},... | collective-permute-start | bytes 86024 | tf_op jit(solution)/shard_map/ppermute | solution.py:20
  9.1 3.3 %collective-permute-start.3 = (bf16[2,7168]{1,0:T(2,128)(2,1)S(1)}, bf16[2,7168]{1,0:T(2,128)(2,1)S(1)}, u32[]{:S(2)}, u32[]{:S(2)}) collective-permute-start(bf16[2,7168]{1,0:T(2,128)(2,1)S(1)} %pad_maximum_fusion.refs_0_), channel_id=1, source_target_pairs={{0,10},{1,11},{2,8},{3,9},{4,14},{5,15},{6,12},{7,13},{8,2},{9,3},... | collective-permute-start | bytes 86024 | tf_op jit(solution)/shard_map/ppermute | solution.py:20
  9.3 3.3 %collective-permute-start.2 = (bf16[2,7168]{1,0:T(2,128)(2,1)S(1)}, bf16[2,7168]{1,0:T(2,128)(2,1)S(1)}, u32[]{:S(2)}, u32[]{:S(2)}) collective-permute-start(bf16[2,7168]{1,0:T(2,128)(2,1)S(1)} %pad_maximum_fusion.refs_0_), channel_id=1, source_target_pairs={{0,9},{1,8},{2,11},{3,10},{4,13},{5,12},{6,15},{7,14},{8,1},{9,0},... | collective-permute-start | bytes 86024 | tf_op jit(solution)/shard_map/ppermute | solution.py:20
  13.7 4.3 %collective-permute-start.7 = (bf16[2,7168]{1,0:T(2,128)(2,1)S(1)}, bf16[2,7168]{1,0:T(2,128)(2,1)S(1)}, u32[]{:S(2)}, u32[]{:S(2)}) collective-permute-start(bf16[2,7168]{1,0:T(2,128)(2,1)S(1)} %get-tuple-element.38), channel_id=1, source_target_pairs={{0,11},{1,10},{2,9},{3,8},{4,15},{5,14},{6,13},{7,12},{8,3},{9,2},... | collective-permute-start | bytes 86024 | tf_op jit(solution)/shard_map/ppermute | solution.py:20
  15.2 3.3 %collective-permute-start.8 = (bf16[2,7168]{1,0:T(2,128)(2,1)S(1)}, bf16[2,7168]{1,0:T(2,128)(2,1)S(1)}, u32[]{:S(2)}, u32[]{:S(2)}) collective-permute-start(bf16[2,7168]{1,0:T(2,128)(2,1)S(1)} %get-tuple-element.39), channel_id=1, source_target_pairs={{0,10},{1,11},{2,8},{3,9},{4,14},{5,15},{6,12},{7,13},{8,2},{9,3},... | collective-permute-start | bytes 86024 | tf_op jit(solution)/shard_map/ppermute | solution.py:20
  15.5 3.3 %collective-permute-start.9 = (bf16[2,7168]{1,0:T(2,128)(2,1)S(1)}, bf16[2,7168]{1,0:T(2,128)(2,1)S(1)}, u32[]{:S(2)}, u32[]{:S(2)}) collective-permute-start(bf16[2,7168]{1,0:T(2,128)(2,1)S(1)} %get-tuple-element.40), channel_id=1, source_target_pairs={{0,9},{1,8},{2,11},{3,10},{4,13},{5,12},{6,15},{7,14},{8,1},{9,0},... | collective-permute-start | bytes 86024 | tf_op jit(solution)/shard_map/ppermute | solution.py:20
  18.9 4.3 %collective-permute-start.10 = (bf16[1,7168]{1,0:T(2,128)(2,1)S(1)}, bf16[1,7168]{1,0:T(2,128)(2,1)S(1)}, u32[]{:S(2)}, u32[]{:S(2)}) collective-permute-start(bf16[1,7168]{1,0:T(2,128)(2,1)S(1)} %slice.15), channel_id=1, source_target_pairs={{0,12},{1,13},{2,14},{3,15},{4,8},{5,9},{6,10},{7,11},{8,4},{9,5},... | collective-permute-start | bytes 43016 | tf_op jit(solution)/shard_map/ppermute | solution.py:20

commit v5 on v4

--- a/solution.py
+++ b/solution.py
@@ -72,10 +72,9 @@
     width = gate_ref.shape[0]
     near = pl.multiple_of(half * width, 128)
     far = pl.multiple_of((1 - half) * width, 128)
-    for k, ref in enumerate(row_refs):
-        rows_scr[k * chunk:(k + 1) * chunk, :] = ref[...].astype(jnp.float32)
-    x_near = rows_scr[:, pl.ds(near, width)].astype(jnp.bfloat16)
-    x_far = rows_scr[:, pl.ds(far, width)].astype(jnp.bfloat16)
+    rows_scr[...] = jnp.concatenate([ref[...] for ref in row_refs], axis=0)
+    x_near = rows_scr[:, pl.ds(near, width)]
+    x_far = rows_scr[:, pl.ds(far, width)]
     gate_pre = dot(x_near, gate_ref[...]) + dot(x_far, gate_far_ref[...])
     up_pre = dot(x_near, up_ref[...]) + dot(x_far, up_far_ref[...])
     hidden = (gate_pre / (1.0 + jnp.exp(-gate_pre)) * up_pre).astype(jnp.bfloat16)
@@ -108,22 +107,22 @@
 def body(tokens, gate_weight, up_weight, down_weight, steering, block_rows, block_gates):
     count = lax.axis_size("ep")
     width_all = tokens.shape[1]
-    here = None
-    pieces = [tokens]
+    here = stage(gate_weight, up_weight, down_weight)
+    own_row, *tables = stage(tokens, steering, block_rows, block_gates)
+    rows = tokens
     owners = [(0, 0)]
     steps = stages(count)
     for i, hops in enumerate(steps):
-        rows = jnp.concatenate(pieces, axis=0) if len(pieces) > 1 else pieces[0]
-        if i == 1:
-            here = stage(gate_weight, up_weight, down_weight, steering, block_rows, block_gates)
-            far = {n: swap_cores(w) for n, w in zip("gud", (gate_weight, up_weight, down_weight))}
-            rows, here, early = lax.optimization_barrier((rows, here, [far[n] for n in "g"]))
-            far.update(zip("g", early))
-        pieces = [rows] + [exchange(rows, d, c) for d, c in hops]
+        got = [exchange(rows, d, c) for d, c in hops]
+        if not i:
+            own_row, got[0], down_weight = lax.optimization_barrier((own_row, got[0], down_weight))
+            far = [swap_cores(w) for w in (gate_weight, up_weight, down_weight)]
+            own_row, got[0], far[0] = lax.optimization_barrier((own_row, got[0], far[0]))
+            rows = own_row
+        pieces = [rows] + got
         owners = owners + [(o ^ d, c ^ x) for d, x in hops for o, c in owners]
-    if here is None:
-        here = stage(gate_weight, up_weight, down_weight, steering, block_rows, block_gates)
-    far = [far[n] for n in "gud"]
+        if i + 1 < len(steps):
+            rows = jnp.concatenate(pieces, axis=0)
     chunk = count // len(pieces)
     vmem = pl.BlockSpec(memory_space=pltpu.VMEM)
     outs = pl.pallas_call(
@@ -132,19 +131,19 @@
         + [jax.ShapeDtypeStruct((chunk, width_all), jnp.bfloat16)] * (len(pieces) - 1),
         in_specs=[vmem] * (len(pieces) + 9),
         out_specs=[vmem] * len(pieces),
-        scratch_shapes=[pltpu.VMEM((count, width_all), jnp.float32), pltpu.VMEM((count, width_all), jnp.float32)],
+        scratch_shapes=[pltpu.VMEM((count, width_all), jnp.bfloat16), pltpu.VMEM((count, width_all), jnp.float32)],
         compiler_params=pltpu.CompilerParams(vmem_limit_bytes=VMEM_LIMIT),
         name="experts",
-    )(*pieces, *here, *far)
+    )(*pieces, *here, *tables, *far)
     total, sends = outs[0], list(outs[1:])
     for i, hops in enumerate(reversed(steps)):
         if i:
             chunk = total.shape[0] // (len(hops) + 1)
-            sends = [total[(k + 1) * chunk:(k + 2) * chunk].astype(jnp.bfloat16) for k in range(len(hops))]
+            sends = [total[(k + 1) * chunk:(k + 2) * chunk].astype(jnp.bfloat16).reshape(8, -1) for k in range(len(hops))]
             total = total[:chunk]
         got = [exchange(s, d, c) for s, (d, c) in reversed(list(zip(sends, hops)))]
         for g in got:
-            total = total + g.astype(jnp.float32)
+            total = total + g.astype(jnp.float32).reshape(total.shape)
     return total.astype(jnp.bfloat16)
 
 

time: 24 us -> 23.7 us (0.987)
  waiting for transfers between devices: 6.76 us -> 5.57 us
  Pallas kernels: 2.79 us -> 3.55 us
    ppermute x8, waiting for transfers between devices: 6.75 us -> 5.56 us  [exchange(): return lax.ppermute(x, ('fsdp', 'ep'), pairs)]
    pallas_call x1 -> x2, Pallas kernels: 1.79 us -> 2.57 us  [stage(): pl.pallas_call(stage_kernel, out_shape=[jax.ShapeDtypeStruct(a.shape, a.d...]
    ppermute x3, starting transfers between devices: 0.96 us -> 0.57 us  [swap_cores(): return lax.ppermute(x, 'fsdp', [(0, 1), (1, 0)])]
    ppermute x8, starting transfers between devices: 12.5 us -> 12.8 us  [exchange(): return lax.ppermute(x, ('fsdp', 'ep'), pairs)]
  transfers between devices with their start and end apart: 11 -> 11, of which waited for: 7 -> 7; matrix products, arithmetic and copies ran while one was open for 0% -> 0% of each run, Pallas kernels for 8% -> 11%
where the time goes in v5:
time: 23.7 us; the launch traced here: 23.5 us
  starting transfers between devices  13.3 us (56%)
  waiting for transfers between devices  5.57 us (24%)
  Pallas kernels  3.55 us (15%)
  other arithmetic  0.77 us (3%)
    ppermute x8, starting transfers between devices, exchange(): return lax.ppermute(x, ('fsdp', 'ep'), pairs)  12.8 us
    ppermute x8, waiting for transfers between devices, exchange(): return lax.ppermute(x, ('fsdp', 'ep'), pairs)  5.56 us
    pallas_call x2, Pallas kernels, stage(): pl.pallas_call(stage_kernel, out_shape=[jax.ShapeDtypeStruct(a.shape, a.d...  2.57 us
    pallas_call x1, Pallas kernels, body(): pl.pallas_call(functools.partial(experts_kernel, owners, len(pieces)), ou...  0.98 us
    convert_element_type x1, other arithmetic, body(): return total.astype(jnp.bfloat16)  0.64 us
    ppermute x3, starting transfers between devices, swap_cores(): return lax.ppermute(x, 'fsdp', [(0, 1), (1, 0)])  0.57 us
  transfers between devices with their start and end apart: 11, of which 7 were waited for; matrix products, arithmetic and copies ran while one was open for 0% of the time, Pallas kernels for 11%

profile of v5, /device:TPU:0, one launch (start us, length us, event | category | flops | bytes accessed | tf_op | source)
XLA Modules:
  0.0 23.5 jit_solution(10467114999959496013)
XLA Ops:
  0.0 0.5 %collective-permute-start.1 = (bf16[3584,128]{1,0:T(8,128)(2,1)}, bf16[3584,128]{1,0:T(8,128)(2,1)S(1)}, u32[]{:S(2)}, u32[]{:S(2)}) collective-permute-start(bf16[3584,128]{1,0:T(8,128)(2,1)} %refs_0_.3), channel_id=1, source_target_pairs={{0,8},{8,0},{1,9},{9,1},{2,10},{10,2},{3,11},{11,3},{4,12},{12,4},... | collective-permute-start | bytes 2752520 | tf_op jit(solution)/shard_map/ppermute | solution.py:14
  0.5 3.7 %collective-permute-start = (bf16[1,7168]{1,0:T(2,128)(2,1)}, bf16[1,7168]{1,0:T(2,128)(2,1)S(1)}, u32[]{:S(2)}, u32[]{:S(2)}) collective-permute-start(bf16[1,7168]{1,0:T(2,128)(2,1)} %refs_0_.2), channel_id=1, source_target_pairs={{0,12},{1,13},{2,14},{3,15},{4,8},{5,9},{6,10},{7,11},{8,4},{9,5},... | collective-permute-start | bytes 43016 | tf_op jit(solution)/shard_map/ppermute | solution.py:20
  4.2 0.0 collective-permute-start.5
  4.2 0.8 %stage.2 = (bf16[1,7168]{1,0:T(2,128)(2,1)S(1)}, bf16[1,7168]{1,0:T(2,128)(2,1)S(1)}, s32[2,1,8]{2,1,0:T(1,128)S(1)}, f32[2,1,8]{2,1,0:T(1,128)S(1)}) custom-call(bf16[1,7168]{1,0:T(2,128)(2,1)} %refs_0_.2, bf16[1,7168]{1,0:T(2,128)(2,1)} %refs_1_.2, s32[2,1,8]{2,1,0:T(1,128)} %refs_2_.2, f32[2,1,8]{2,1,0:T(1,128)} %refs_3_.1), custom_call_target="tpu_custom_call" | custom-call | tf_op jit(solution)/shard_map/stage/pallas_call | solution.py:49
  5.0 1.1 %collective-permute-done = bf16[1,7168]{1,0:T(2,128)(2,1)S(1)} collective-permute-done((bf16[1,7168]{1,0:T(2,128)(2,1)}, bf16[1,7168]{1,0:T(2,128)(2,1)S(1)}, u32[]{:S(2)}, u32[]{:S(2)}) %collective-permute-start) | collective-permute-done | bytes 14368 | tf_op jit(solution)/shard_map/ppermute | solution.py:20
  6.0 0.1 collective-permute-start.6
  6.2 0.0 collective-permute-done.1.refs_10_
  6.2 0.1 pad_maximum_fusion.refs_0_
  6.2 2.5 %collective-permute-start.4 = (bf16[2,7168]{1,0:T(2,128)(2,1)S(1)}, bf16[2,7168]{1,0:T(2,128)(2,1)S(1)}, u32[]{:S(2)}, u32[]{:S(2)}) collective-permute-start(bf16[2,7168]{1,0:T(2,128)(2,1)S(1)} %pad_maximum_fusion.refs_0_), channel_id=1, source_target_pairs={{0,11},{1,10},{2,9},{3,8},{4,15},{5,14},{6,13},{7,12},{8,3},{9,2},... | collective-permute-start | bytes 86024 | tf_op jit(solution)/shard_map/ppermute | solution.py:20
  8.7 0.4 %collective-permute-start.3 = (bf16[2,7168]{1,0:T(2,128)(2,1)S(1)}, bf16[2,7168]{1,0:T(2,128)(2,1)S(1)}, u32[]{:S(2)}, u32[]{:S(2)}) collective-permute-start(bf16[2,7168]{1,0:T(2,128)(2,1)S(1)} %pad_maximum_fusion.refs_0_), channel_id=1, source_target_pairs={{0,10},{1,11},{2,8},{3,9},{4,14},{5,15},{6,12},{7,13},{8,2},{9,3},... | collective-permute-start | bytes 86024 | tf_op jit(solution)/shard_map/ppermute | solution.py:20
  9.2 0.3 %collective-permute-start.2 = (bf16[2,7168]{1,0:T(2,128)(2,1)S(1)}, bf16[2,7168]{1,0:T(2,128)(2,1)S(1)}, u32[]{:S(2)}, u32[]{:S(2)}) collective-permute-start(bf16[2,7168]{1,0:T(2,128)(2,1)S(1)} %pad_maximum_fusion.refs_0_), channel_id=1, source_target_pairs={{0,9},{1,8},{2,11},{3,10},{4,13},{5,12},{6,15},{7,14},{8,1},{9,0},... | collective-permute-start | bytes 86024 | tf_op jit(solution)/shard_map/ppermute | solution.py:20
  9.5 1.8 %stage.3 = (bf16[3584,128]{1,0:T(8,128)(2,1)S(1)}, bf16[3584,128]{1,0:T(8,128)(2,1)S(1)}, bf16[128,3584]{1,0:T(8,128)(2,1)S(1)}) custom-call(bf16[3584,128]{1,0:T(8,128)(2,1)} %refs_0_.3, bf16[3584,128]{1,0:T(8,128)(2,1)} %refs_1_.3, bf16[128,3584]{1,0:T(8,128)(2,1)} %refs_2_.3), custom_call_target="tpu_custom_call" | custom-call | tf_op jit(solution)/shard_map/stage/pallas_call | solution.py:49
  11.3 0.0 collective-permute-done.5.refs_11_
  11.3 0.0 collective-permute-done.6.refs_12_
  11.3 0.0 collective-permute-done.4.refs_3_
  11.3 0.8 %collective-permute-done.3.refs_2_ = bf16[2,7168]{1,0:T(2,128)(2,1)S(1)} collective-permute-done((bf16[2,7168]{1,0:T(2,128)(2,1)S(1)}, bf16[2,7168]{1,0:T(2,128)(2,1)S(1)}, u32[]{:S(2)}, u32[]{:S(2)}) %collective-permute-start.3) | collective-permute-done | bytes 28704 | tf_op jit(solution)/shard_map/ppermute | solution.py:20
  12.1 0.5 %collective-permute-done.2.refs_1_ = bf16[2,7168]{1,0:T(2,128)(2,1)S(1)} collective-permute-done((bf16[2,7168]{1,0:T(2,128)(2,1)S(1)}, bf16[2,7168]{1,0:T(2,128)(2,1)S(1)}, u32[]{:S(2)}, u32[]{:S(2)}) %collective-permute-start.2) | collective-permute-done | bytes 28704 | tf_op jit(solution)/shard_map/ppermute | solution.py:20
  12.5 1.0 %experts.1 = (f32[2,7168]{1,0:T(2,128)S(1)}, bf16[2,7168]{1,0:T(2,128)(2,1)S(1)}, bf16[2,7168]{1,0:T(2,128)(2,1)S(1)}, bf16[2,7168]{1,0:T(2,128)(2,1)S(1)}) custom-call(bf16[2,7168]{1,0:T(2,128)(2,1)S(1)} %pad_maximum_fusion.refs_0_, bf16[2,7168]{1,0:T(2,128)(2,1)S(1)} %collective-permute-done.2.refs_1_, bf16[2,7168]{1,0:T(2,128)(2,1)S(1)} %collective-permute-done.3.refs_2_, ...), custom_call_target="tpu_custom_call" | custom-call | tf_op jit(solution)/shard_map/experts/pallas_call | solution.py:128
  13.5 1.4 %collective-permute-start.7 = (bf16[2,7168]{1,0:T(2,128)(2,1)S(1)}, bf16[2,7168]{1,0:T(2,128)(2,1)S(1)}, u32[]{:S(2)}, u32[]{:S(2)}) collective-permute-start(bf16[2,7168]{1,0:T(2,128)(2,1)S(1)} %get-tuple-element.36), channel_id=1, source_target_pairs={{0,11},{1,10},{2,9},{3,8},{4,15},{5,14},{6,13},{7,12},{8,3},{9,2},... | collective-permute-start | bytes 86024 | tf_op jit(solution)/shard_map/ppermute | solution.py:20
  14.9 0.2 collective-permute-start.8
  15.1 1.5 %collective-permute-start.9 = (bf16[2,7168]{1,0:T(2,128)(2,1)S(1)}, bf16[2,7168]{1,0:T(2,128)(2,1)S(1)}, u32[]{:S(2)}, u32[]{:S(2)}) collective-permute-start(bf16[2,7168]{1,0:T(2,128)(2,1)S(1)} %get-tuple-element.38), channel_id=1, source_target_pairs={{0,9},{1,8},{2,11},{3,10},{4,13},{5,12},{6,15},{7,14},{8,1},{9,0},... | collective-permute-start | bytes 86024 | tf_op jit(solution)/shard_map/ppermute | solution.py:20
  16.5 1.2 %collective-permute-done.7 = bf16[2,7168]{1,0:T(2,128)(2,1)S(1)} collective-permute-done((bf16[2,7168]{1,0:T(2,128)(2,1)S(1)}, bf16[2,7168]{1,0:T(2,128)(2,1)S(1)}, u32[]{:S(2)}, u32[]{:S(2)}) %collective-permute-start.7) | collective-permute-done | bytes 28704 | tf_op jit(solution)/shard_map/ppermute | solution.py:20
  17.8 0.4 %collective-permute-done.8 = bf16[2,7168]{1,0:T(2,128)(2,1)S(1)} collective-permute-done((bf16[2,7168]{1,0:T(2,128)(2,1)S(1)}, bf16[2,7168]{1,0:T(2,128)(2,1)S(1)}, u32[]{:S(2)}, u32[]{:S(2)}) %collective-permute-start.8) | collective-permute-done | bytes 28704 | tf_op jit(solution)/shard_map/ppermute | solution.py:20
  18.2 0.2 collective-permute-done.9
  18.4 0.1 convert_add_fusion
  18.5 0.1 fusion
  18.6 2.8 %collective-permute-start.10 = (bf16[8,896]{1,0:T(8,128)(2,1)S(1)}, bf16[8,896]{1,0:T(8,128)(2,1)S(1)}, u32[]{:S(2)}, u32[]{:S(2)}) collective-permute-start(bf16[8,896]{1,0:T(8,128)(2,1)S(1)} %reshape.9), channel_id=1, source_target_pairs={{0,12},{1,13},{2,14},{3,15},{4,8},{5,9},{6,10},{7,11},{8,4},{9,5},... | collective-permute-start | bytes 43016 | tf_op jit(solution)/shard_map/ppermute | solution.py:20
  21.4 1.4 %collective-permute-done.10 = bf16[8,896]{1,0:T(8,128)(2,1)S(1)} collective-permute-done((bf16[8,896]{1,0:T(8,128)(2,1)S(1)}, bf16[8,896]{1,0:T(8,128)(2,1)S(1)}, u32[]{:S(2)}, u32[]{:S(2)}) %collective-permute-start.10) | collective-permute-done | bytes 14368 | tf_op jit(solution)/shard_map/ppermute | solution.py:20
  22.8 0.6 %fusion.1 = bf16[1,7168]{1,0:T(2,128)(2,1)} fusion(f32[1,7168]{1,0:T(1,128)S(1)} %bitcast.4, f32[2,7168]{1,0:T(2,128)S(1)} %convert_add_fusion), kind=kLoop, calls=%fused_computation.4 | loop fusion | flops 14336 | bytes 71680 | tf_op jit(solution)/shard_map/convert_element_type | solution.py:147
  (3 shorter events, 0.1 us)
Async XLA Ops:
  0.0 6.2 %collective-permute-start.1 = (bf16[3584,128]{1,0:T(8,128)(2,1)}, bf16[3584,128]{1,0:T(8,128)(2,1)S(1)}, u32[]{:S(2)}, u32[]{:S(2)}) collective-permute-start(bf16[3584,128]{1,0:T(8,128)(2,1)} %refs_0_.3), channel_id=1, source_target_pairs={{0,8},{8,0},{1,9},{9,1},{2,10},{10,2},{3,11},{11,3},{4,12},{12,4},... | collective-permute-start | bytes 2752520 | tf_op jit(solution)/shard_map/ppermute | solution.py:14
  0.5 5.6 %collective-permute-start = (bf16[1,7168]{1,0:T(2,128)(2,1)}, bf16[1,7168]{1,0:T(2,128)(2,1)S(1)}, u32[]{:S(2)}, u32[]{:S(2)}) collective-permute-start(bf16[1,7168]{1,0:T(2,128)(2,1)} %refs_0_.2), channel_id=1, source_target_pairs={{0,12},{1,13},{2,14},{3,15},{4,8},{5,9},{6,10},{7,11},{8,4},{9,5},... | collective-permute-start | bytes 43016 | tf_op jit(solution)/shard_map/ppermute | solution.py:20
  4.2 7.1 %collective-permute-start.5 = (bf16[3584,128]{1,0:T(8,128)(2,1)}, bf16[3584,128]{1,0:T(8,128)(2,1)S(1)}, u32[]{:S(2)}, u32[]{:S(2)}) collective-permute-start(bf16[3584,128]{1,0:T(8,128)(2,1)} %refs_1_.3), channel_id=1, source_target_pairs={{0,8},{8,0},{1,9},{9,1},{2,10},{10,2},{3,11},{11,3},{4,12},{12,4},... | collective-permute-start | bytes 2752520 | tf_op jit(solution)/shard_map/ppermute | solution.py:14
  6.0 5.2 %collective-permute-start.6 = (bf16[128,3584]{1,0:T(8,128)(2,1)}, bf16[128,3584]{1,0:T(8,128)(2,1)S(1)}, u32[]{:S(2)}, u32[]{:S(2)}) collective-permute-start(bf16[128,3584]{1,0:T(8,128)(2,1)} %refs_2_.3), channel_id=1, source_target_pairs={{0,8},{8,0},{1,9},{9,1},{2,10},{10,2},{3,11},{11,3},{4,12},{12,4},... | collective-permute-start | bytes 2752520 | tf_op jit(solution)/shard_map/ppermute | solution.py:14
  6.2 5.1 %collective-permute-start.4 = (bf16[2,7168]{1,0:T(2,128)(2,1)S(1)}, bf16[2,7168]{1,0:T(2,128)(2,1)S(1)}, u32[]{:S(2)}, u32[]{:S(2)}) collective-permute-start(bf16[2,7168]{1,0:T(2,128)(2,1)S(1)} %pad_maximum_fusion.refs_0_), channel_id=1, source_target_pairs={{0,11},{1,10},{2,9},{3,8},{4,15},{5,14},{6,13},{7,12},{8,3},{9,2},... | collective-permute-start | bytes 86024 | tf_op jit(solution)/shard_map/ppermute | solution.py:20
  8.7 3.3 %collective-permute-start.3 = (bf16[2,7168]{1,0:T(2,128)(2,1)S(1)}, bf16[2,7168]{1,0:T(2,128)(2,1)S(1)}, u32[]{:S(2)}, u32[]{:S(2)}) collective-permute-start(bf16[2,7168]{1,0:T(2,128)(2,1)S(1)} %pad_maximum_fusion.refs_0_), channel_id=1, source_target_pairs={{0,10},{1,11},{2,8},{3,9},{4,14},{5,15},{6,12},{7,13},{8,2},{9,3},... | collective-permute-start | bytes 86024 | tf_op jit(solution)/shard_map/ppermute | solution.py:20
  9.2 3.4 %collective-permute-start.2 = (bf16[2,7168]{1,0:T(2,128)(2,1)S(1)}, bf16[2,7168]{1,0:T(2,128)(2,1)S(1)}, u32[]{:S(2)}, u32[]{:S(2)}) collective-permute-start(bf16[2,7168]{1,0:T(2,128)(2,1)S(1)} %pad_maximum_fusion.refs_0_), channel_id=1, source_target_pairs={{0,9},{1,8},{2,11},{3,10},{4,13},{5,12},{6,15},{7,14},{8,1},{9,0},... | collective-permute-start | bytes 86024 | tf_op jit(solution)/shard_map/ppermute | solution.py:20
  13.5 4.3 %collective-permute-start.7 = (bf16[2,7168]{1,0:T(2,128)(2,1)S(1)}, bf16[2,7168]{1,0:T(2,128)(2,1)S(1)}, u32[]{:S(2)}, u32[]{:S(2)}) collective-permute-start(bf16[2,7168]{1,0:T(2,128)(2,1)S(1)} %get-tuple-element.36), channel_id=1, source_target_pairs={{0,11},{1,10},{2,9},{3,8},{4,15},{5,14},{6,13},{7,12},{8,3},{9,2},... | collective-permute-start | bytes 86024 | tf_op jit(solution)/shard_map/ppermute | solution.py:20
  14.9 3.3 %collective-permute-start.8 = (bf16[2,7168]{1,0:T(2,128)(2,1)S(1)}, bf16[2,7168]{1,0:T(2,128)(2,1)S(1)}, u32[]{:S(2)}, u32[]{:S(2)}) collective-permute-start(bf16[2,7168]{1,0:T(2,128)(2,1)S(1)} %get-tuple-element.37), channel_id=1, source_target_pairs={{0,10},{1,11},{2,8},{3,9},{4,14},{5,15},{6,12},{7,13},{8,2},{9,3},... | collective-permute-start | bytes 86024 | tf_op jit(solution)/shard_map/ppermute | solution.py:20
  15.1 3.3 %collective-permute-start.9 = (bf16[2,7168]{1,0:T(2,128)(2,1)S(1)}, bf16[2,7168]{1,0:T(2,128)(2,1)S(1)}, u32[]{:S(2)}, u32[]{:S(2)}) collective-permute-start(bf16[2,7168]{1,0:T(2,128)(2,1)S(1)} %get-tuple-element.38), channel_id=1, source_target_pairs={{0,9},{1,8},{2,11},{3,10},{4,13},{5,12},{6,15},{7,14},{8,1},{9,0},... | collective-permute-start | bytes 86024 | tf_op jit(solution)/shard_map/ppermute | solution.py:20
  18.6 4.2 %collective-permute-start.10 = (bf16[8,896]{1,0:T(8,128)(2,1)S(1)}, bf16[8,896]{1,0:T(8,128)(2,1)S(1)}, u32[]{:S(2)}, u32[]{:S(2)}) collective-permute-start(bf16[8,896]{1,0:T(8,128)(2,1)S(1)} %reshape.9), channel_id=1, source_target_pairs={{0,12},{1,13},{2,14},{3,15},{4,8},{5,9},{6,10},{7,11},{8,4},{9,5},... | collective-permute-start | bytes 43016 | tf_op jit(solution)/shard_map/ppermute | solution.py:20

commit v6 on v5

--- a/solution.py
+++ b/solution.py
@@ -104,6 +104,35 @@
         ref[...] = out_scr[(k + 1) * chunk:(k + 2) * chunk, :].astype(jnp.bfloat16)
 
 
+def combine_kernel(*refs):
+    keep_ref, own_ref, send_ref, scr = refs[0], *refs[-3:]
+    total = keep_ref[...]
+    for ref in refs[1:-3]:
+        total = total + ref[...].astype(jnp.float32)
+    own_ref[...] = total
+    lanes = scr.shape[1]
+    for p in range(scr.shape[0]):
+        scr[p:p + 1, :] = total[1:2, p * lanes:(p + 1) * lanes]
+    send_ref[...] = scr[...].astype(jnp.bfloat16)
+
+
+def combine(keep, got):
+    vmem = pl.BlockSpec(memory_space=pltpu.VMEM)
+    send_shape = (8, keep.shape[1] // 8)
+    return pl.pallas_call(
+        combine_kernel,
+        out_shape=[
+            jax.ShapeDtypeStruct(keep.shape, jnp.float32),
+            jax.ShapeDtypeStruct(send_shape, jnp.bfloat16),
+        ],
+        in_specs=[vmem] * (1 + len(got)),
+        out_specs=[vmem] * 2,
+        scratch_shapes=[pltpu.VMEM(send_shape, jnp.float32)],
+        compiler_params=pltpu.CompilerParams(vmem_limit_bytes=VMEM_LIMIT),
+        name="combine",
+    )(keep, *got)
+
+
 def body(tokens, gate_weight, up_weight, down_weight, steering, block_rows, block_gates):
     count = lax.axis_size("ep")
     width_all = tokens.shape[1]
@@ -136,12 +165,19 @@
         name="experts",
     )(*pieces, *here, *tables, *far)
     total, sends = outs[0], list(outs[1:])
+    ready = None
     for i, hops in enumerate(reversed(steps)):
         if i:
             chunk = total.shape[0] // (len(hops) + 1)
-            sends = [total[(k + 1) * chunk:(k + 2) * chunk].astype(jnp.bfloat16).reshape(8, -1) for k in range(len(hops))]
+            sends = ready or [
+                total[(k + 1) * chunk:(k + 2) * chunk].astype(jnp.bfloat16).reshape(8, -1) for k in range(len(hops))
+            ]
             total = total[:chunk]
         got = [exchange(s, d, c) for s, (d, c) in reversed(list(zip(sends, hops)))]
+        if total.shape[0] == 2 and not i:
+            total, *ready = combine(total, got)
+            continue
+        ready = None
         for g in got:
             total = total + g.astype(jnp.float32).reshape(total.shape)
     return total.astype(jnp.bfloat16)

time: 23.7 us -> 23.5 us (level)
  no operation moved by 1% of the time
where the time goes in v6:
time: 23.5 us; the launch traced here: 23.3 us
  starting transfers between devices  13.3 us (57%)
  waiting for transfers between devices  5.57 us (24%)
  Pallas kernels  3.58 us (15%)
  other arithmetic  0.72 us (3%)
    ppermute x8, starting transfers between devices, exchange(): return lax.ppermute(x, ('fsdp', 'ep'), pairs)  12.8 us
    ppermute x8, waiting for transfers between devices, exchange(): return lax.ppermute(x, ('fsdp', 'ep'), pairs)  5.56 us
    pallas_call x2, Pallas kernels, stage(): pl.pallas_call(stage_kernel, out_shape=[jax.ShapeDtypeStruct(a.shape, a.d...  2.57 us
    pallas_call x1, Pallas kernels, body(): pl.pallas_call(functools.partial(experts_kernel, owners, len(pieces)), ou...  0.98 us
    convert_element_type x1, other arithmetic, body(): return total.astype(jnp.bfloat16)  0.64 us
    ppermute x3, starting transfers between devices, swap_cores(): return lax.ppermute(x, 'fsdp', [(0, 1), (1, 0)])  0.57 us
  transfers between devices with their start and end apart: 11, of which 7 were waited for; matrix products, arithmetic and copies ran while one was open for 0% of the time, Pallas kernels for 11%

profile of v6, /device:TPU:0, one launch (start us, length us, event | category | flops | bytes accessed | tf_op | source)
XLA Modules:
  0.0 23.3 jit_solution(3616141400656890643)
XLA Ops:
  0.0 0.5 %collective-permute-start.1 = (bf16[3584,128]{1,0:T(8,128)(2,1)}, bf16[3584,128]{1,0:T(8,128)(2,1)S(1)}, u32[]{:S(2)}, u32[]{:S(2)}) collective-permute-start(bf16[3584,128]{1,0:T(8,128)(2,1)} %refs_0_.3), channel_id=1, source_target_pairs={{0,8},{8,0},{1,9},{9,1},{2,10},{10,2},{3,11},{11,3},{4,12},{12,4},... | collective-permute-start | bytes 2752520 | tf_op jit(solution)/shard_map/ppermute | solution.py:14
  0.5 3.7 %collective-permute-start = (bf16[1,7168]{1,0:T(2,128)(2,1)}, bf16[1,7168]{1,0:T(2,128)(2,1)S(1)}, u32[]{:S(2)}, u32[]{:S(2)}) collective-permute-start(bf16[1,7168]{1,0:T(2,128)(2,1)} %refs_0_.2), channel_id=1, source_target_pairs={{0,12},{1,13},{2,14},{3,15},{4,8},{5,9},{6,10},{7,11},{8,4},{9,5},... | collective-permute-start | bytes 43016 | tf_op jit(solution)/shard_map/ppermute | solution.py:20
  4.2 0.0 collective-permute-start.5
  4.2 0.8 %stage.2 = (bf16[1,7168]{1,0:T(2,128)(2,1)S(1)}, bf16[1,7168]{1,0:T(2,128)(2,1)S(1)}, s32[2,1,8]{2,1,0:T(1,128)S(1)}, f32[2,1,8]{2,1,0:T(1,128)S(1)}) custom-call(bf16[1,7168]{1,0:T(2,128)(2,1)} %refs_0_.2, bf16[1,7168]{1,0:T(2,128)(2,1)} %refs_1_.2, s32[2,1,8]{2,1,0:T(1,128)} %refs_2_.2, f32[2,1,8]{2,1,0:T(1,128)} %refs_3_.1), custom_call_target="tpu_custom_call" | custom-call | tf_op jit(solution)/shard_map/stage/pallas_call | solution.py:49
  5.0 1.1 %collective-permute-done = bf16[1,7168]{1,0:T(2,128)(2,1)S(1)} collective-permute-done((bf16[1,7168]{1,0:T(2,128)(2,1)}, bf16[1,7168]{1,0:T(2,128)(2,1)S(1)}, u32[]{:S(2)}, u32[]{:S(2)}) %collective-permute-start) | collective-permute-done | bytes 14368 | tf_op jit(solution)/shard_map/ppermute | solution.py:20
  6.0 0.1 collective-permute-start.6
  6.2 0.0 collective-permute-done.1.refs_10_
  6.2 0.1 pad_maximum_fusion.refs_0_
  6.2 2.5 %collective-permute-start.4 = (bf16[2,7168]{1,0:T(2,128)(2,1)S(1)}, bf16[2,7168]{1,0:T(2,128)(2,1)S(1)}, u32[]{:S(2)}, u32[]{:S(2)}) collective-permute-start(bf16[2,7168]{1,0:T(2,128)(2,1)S(1)} %pad_maximum_fusion.refs_0_), channel_id=1, source_target_pairs={{0,11},{1,10},{2,9},{3,8},{4,15},{5,14},{6,13},{7,12},{8,3},{9,2},... | collective-permute-start | bytes 86024 | tf_op jit(solution)/shard_map/ppermute | solution.py:20
  8.7 0.4 %collective-permute-start.3 = (bf16[2,7168]{1,0:T(2,128)(2,1)S(1)}, bf16[2,7168]{1,0:T(2,128)(2,1)S(1)}, u32[]{:S(2)}, u32[]{:S(2)}) collective-permute-start(bf16[2,7168]{1,0:T(2,128)(2,1)S(1)} %pad_maximum_fusion.refs_0_), channel_id=1, source_target_pairs={{0,10},{1,11},{2,8},{3,9},{4,14},{5,15},{6,12},{7,13},{8,2},{9,3},... | collective-permute-start | bytes 86024 | tf_op jit(solution)/shard_map/ppermute | solution.py:20
  9.2 0.3 %collective-permute-start.2 = (bf16[2,7168]{1,0:T(2,128)(2,1)S(1)}, bf16[2,7168]{1,0:T(2,128)(2,1)S(1)}, u32[]{:S(2)}, u32[]{:S(2)}) collective-permute-start(bf16[2,7168]{1,0:T(2,128)(2,1)S(1)} %pad_maximum_fusion.refs_0_), channel_id=1, source_target_pairs={{0,9},{1,8},{2,11},{3,10},{4,13},{5,12},{6,15},{7,14},{8,1},{9,0},... | collective-permute-start | bytes 86024 | tf_op jit(solution)/shard_map/ppermute | solution.py:20
  9.5 1.8 %stage.3 = (bf16[3584,128]{1,0:T(8,128)(2,1)S(1)}, bf16[3584,128]{1,0:T(8,128)(2,1)S(1)}, bf16[128,3584]{1,0:T(8,128)(2,1)S(1)}) custom-call(bf16[3584,128]{1,0:T(8,128)(2,1)} %refs_0_.3, bf16[3584,128]{1,0:T(8,128)(2,1)} %refs_1_.3, bf16[128,3584]{1,0:T(8,128)(2,1)} %refs_2_.3), custom_call_target="tpu_custom_call" | custom-call | tf_op jit(solution)/shard_map/stage/pallas_call | solution.py:49
  11.3 0.0 collective-permute-done.5.refs_11_
  11.3 0.0 collective-permute-done.6.refs_12_
  11.3 0.0 collective-permute-done.4.refs_3_
  11.3 0.8 %collective-permute-done.3.refs_2_ = bf16[2,7168]{1,0:T(2,128)(2,1)S(1)} collective-permute-done((bf16[2,7168]{1,0:T(2,128)(2,1)S(1)}, bf16[2,7168]{1,0:T(2,128)(2,1)S(1)}, u32[]{:S(2)}, u32[]{:S(2)}) %collective-permute-start.3) | collective-permute-done | bytes 28704 | tf_op jit(solution)/shard_map/ppermute | solution.py:20
  12.1 0.5 %collective-permute-done.2.refs_1_ = bf16[2,7168]{1,0:T(2,128)(2,1)S(1)} collective-permute-done((bf16[2,7168]{1,0:T(2,128)(2,1)S(1)}, bf16[2,7168]{1,0:T(2,128)(2,1)S(1)}, u32[]{:S(2)}, u32[]{:S(2)}) %collective-permute-start.2) | collective-permute-done | bytes 28704 | tf_op jit(solution)/shard_map/ppermute | solution.py:20
  12.5 1.0 %experts.1 = (f32[2,7168]{1,0:T(2,128)S(1)}, bf16[2,7168]{1,0:T(2,128)(2,1)S(1)}, bf16[2,7168]{1,0:T(2,128)(2,1)S(1)}, bf16[2,7168]{1,0:T(2,128)(2,1)S(1)}) custom-call(bf16[2,7168]{1,0:T(2,128)(2,1)S(1)} %pad_maximum_fusion.refs_0_, bf16[2,7168]{1,0:T(2,128)(2,1)S(1)} %collective-permute-done.2.refs_1_, bf16[2,7168]{1,0:T(2,128)(2,1)S(1)} %collective-permute-done.3.refs_2_, ...), custom_call_target="tpu_custom_call" | custom-call | tf_op jit(solution)/shard_map/experts/pallas_call | solution.py:157
  13.5 1.4 %collective-permute-start.7 = (bf16[2,7168]{1,0:T(2,128)(2,1)S(1)}, bf16[2,7168]{1,0:T(2,128)(2,1)S(1)}, u32[]{:S(2)}, u32[]{:S(2)}) collective-permute-start(bf16[2,7168]{1,0:T(2,128)(2,1)S(1)} %get-tuple-element.38), channel_id=1, source_target_pairs={{0,11},{1,10},{2,9},{3,8},{4,15},{5,14},{6,13},{7,12},{8,3},{9,2},... | collective-permute-start | bytes 86024 | tf_op jit(solution)/shard_map/ppermute | solution.py:20
  14.9 0.2 collective-permute-start.8
  15.1 1.5 %collective-permute-start.9 = (bf16[2,7168]{1,0:T(2,128)(2,1)S(1)}, bf16[2,7168]{1,0:T(2,128)(2,1)S(1)}, u32[]{:S(2)}, u32[]{:S(2)}) collective-permute-start(bf16[2,7168]{1,0:T(2,128)(2,1)S(1)} %get-tuple-element.40), channel_id=1, source_target_pairs={{0,9},{1,8},{2,11},{3,10},{4,13},{5,12},{6,15},{7,14},{8,1},{9,0},... | collective-permute-start | bytes 86024 | tf_op jit(solution)/shard_map/ppermute | solution.py:20
  16.5 1.2 %collective-permute-done.7.refs_1_ = bf16[2,7168]{1,0:T(2,128)(2,1)S(1)} collective-permute-done((bf16[2,7168]{1,0:T(2,128)(2,1)S(1)}, bf16[2,7168]{1,0:T(2,128)(2,1)S(1)}, u32[]{:S(2)}, u32[]{:S(2)}) %collective-permute-start.7) | collective-permute-done | bytes 28704 | tf_op jit(solution)/shard_map/ppermute | solution.py:20
  17.8 0.4 %collective-permute-done.8.refs_2_ = bf16[2,7168]{1,0:T(2,128)(2,1)S(1)} collective-permute-done((bf16[2,7168]{1,0:T(2,128)(2,1)S(1)}, bf16[2,7168]{1,0:T(2,128)(2,1)S(1)}, u32[]{:S(2)}, u32[]{:S(2)}) %collective-permute-start.8) | collective-permute-done | bytes 28704 | tf_op jit(solution)/shard_map/ppermute | solution.py:20
  18.2 0.2 collective-permute-done.9.refs_3_
  18.4 2.8 %collective-permute-start.10 = (bf16[8,896]{1,0:T(8,128)(2,1)S(1)}, bf16[8,896]{1,0:T(8,128)(2,1)S(1)}, u32[]{:S(2)}, u32[]{:S(2)}) collective-permute-start(bf16[8,896]{1,0:T(8,128)(2,1)S(1)} %get-tuple-element.42), channel_id=1, source_target_pairs={{0,12},{1,13},{2,14},{3,15},{4,8},{5,9},{6,10},{7,11},{8,4},{9,5},... | collective-permute-start | bytes 43016 | tf_op jit(solution)/shard_map/ppermute | solution.py:20
  21.2 1.4 %collective-permute-done.10 = bf16[8,896]{1,0:T(8,128)(2,1)S(1)} collective-permute-done((bf16[8,896]{1,0:T(8,128)(2,1)S(1)}, bf16[8,896]{1,0:T(8,128)(2,1)S(1)}, u32[]{:S(2)}, u32[]{:S(2)}) %collective-permute-start.10) | collective-permute-done | bytes 14368 | tf_op jit(solution)/shard_map/ppermute | solution.py:20
  22.7 0.6 %add_convert_fusion = bf16[1,7168]{1,0:T(2,128)(2,1)} fusion(f32[1,7168]{1,0:T(1,128)S(1)} %bitcast.4, f32[2,7168]{1,0:T(2,128)S(1)} %get-tuple-element.41), kind=kLoop, calls=%fused_computation.2 | loop fusion | flops 14336 | bytes 71680 | tf_op jit(solution)/shard_map/convert_element_type | solution.py:183
  (3 shorter events, 0.1 us)
Async XLA Ops:
  0.0 6.2 %collective-permute-start.1 = (bf16[3584,128]{1,0:T(8,128)(2,1)}, bf16[3584,128]{1,0:T(8,128)(2,1)S(1)}, u32[]{:S(2)}, u32[]{:S(2)}) collective-permute-start(bf16[3584,128]{1,0:T(8,128)(2,1)} %refs_0_.3), channel_id=1, source_target_pairs={{0,8},{8,0},{1,9},{9,1},{2,10},{10,2},{3,11},{11,3},{4,12},{12,4},... | collective-permute-start | bytes 2752520 | tf_op jit(solution)/shard_map/ppermute | solution.py:14
  0.5 5.6 %collective-permute-start = (bf16[1,7168]{1,0:T(2,128)(2,1)}, bf16[1,7168]{1,0:T(2,128)(2,1)S(1)}, u32[]{:S(2)}, u32[]{:S(2)}) collective-permute-start(bf16[1,7168]{1,0:T(2,128)(2,1)} %refs_0_.2), channel_id=1, source_target_pairs={{0,12},{1,13},{2,14},{3,15},{4,8},{5,9},{6,10},{7,11},{8,4},{9,5},... | collective-permute-start | bytes 43016 | tf_op jit(solution)/shard_map/ppermute | solution.py:20
  4.2 7.1 %collective-permute-start.5 = (bf16[3584,128]{1,0:T(8,128)(2,1)}, bf16[3584,128]{1,0:T(8,128)(2,1)S(1)}, u32[]{:S(2)}, u32[]{:S(2)}) collective-permute-start(bf16[3584,128]{1,0:T(8,128)(2,1)} %refs_1_.3), channel_id=1, source_target_pairs={{0,8},{8,0},{1,9},{9,1},{2,10},{10,2},{3,11},{11,3},{4,12},{12,4},... | collective-permute-start | bytes 2752520 | tf_op jit(solution)/shard_map/ppermute | solution.py:14
  6.0 5.2 %collective-permute-start.6 = (bf16[128,3584]{1,0:T(8,128)(2,1)}, bf16[128,3584]{1,0:T(8,128)(2,1)S(1)}, u32[]{:S(2)}, u32[]{:S(2)}) collective-permute-start(bf16[128,3584]{1,0:T(8,128)(2,1)} %refs_2_.3), channel_id=1, source_target_pairs={{0,8},{8,0},{1,9},{9,1},{2,10},{10,2},{3,11},{11,3},{4,12},{12,4},... | collective-permute-start | bytes 2752520 | tf_op jit(solution)/shard_map/ppermute | solution.py:14
  6.2 5.1 %collective-permute-start.4 = (bf16[2,7168]{1,0:T(2,128)(2,1)S(1)}, bf16[2,7168]{1,0:T(2,128)(2,1)S(1)}, u32[]{:S(2)}, u32[]{:S(2)}) collective-permute-start(bf16[2,7168]{1,0:T(2,128)(2,1)S(1)} %pad_maximum_fusion.refs_0_), channel_id=1, source_target_pairs={{0,11},{1,10},{2,9},{3,8},{4,15},{5,14},{6,13},{7,12},{8,3},{9,2},... | collective-permute-start | bytes 86024 | tf_op jit(solution)/shard_map/ppermute | solution.py:20
  8.7 3.3 %collective-permute-start.3 = (bf16[2,7168]{1,0:T(2,128)(2,1)S(1)}, bf16[2,7168]{1,0:T(2,128)(2,1)S(1)}, u32[]{:S(2)}, u32[]{:S(2)}) collective-permute-start(bf16[2,7168]{1,0:T(2,128)(2,1)S(1)} %pad_maximum_fusion.refs_0_), channel_id=1, source_target_pairs={{0,10},{1,11},{2,8},{3,9},{4,14},{5,15},{6,12},{7,13},{8,2},{9,3},... | collective-permute-start | bytes 86024 | tf_op jit(solution)/shard_map/ppermute | solution.py:20
  9.2 3.4 %collective-permute-start.2 = (bf16[2,7168]{1,0:T(2,128)(2,1)S(1)}, bf16[2,7168]{1,0:T(2,128)(2,1)S(1)}, u32[]{:S(2)}, u32[]{:S(2)}) collective-permute-start(bf16[2,7168]{1,0:T(2,128)(2,1)S(1)} %pad_maximum_fusion.refs_0_), channel_id=1, source_target_pairs={{0,9},{1,8},{2,11},{3,10},{4,13},{5,12},{6,15},{7,14},{8,1},{9,0},... | collective-permute-start | bytes 86024 | tf_op jit(solution)/shard_map/ppermute | solution.py:20
  13.5 4.3 %collective-permute-start.7 = (bf16[2,7168]{1,0:T(2,128)(2,1)S(1)}, bf16[2,7168]{1,0:T(2,128)(2,1)S(1)}, u32[]{:S(2)}, u32[]{:S(2)}) collective-permute-start(bf16[2,7168]{1,0:T(2,128)(2,1)S(1)} %get-tuple-element.38), channel_id=1, source_target_pairs={{0,11},{1,10},{2,9},{3,8},{4,15},{5,14},{6,13},{7,12},{8,3},{9,2},... | collective-permute-start | bytes 86024 | tf_op jit(solution)/shard_map/ppermute | solution.py:20
  14.9 3.3 %collective-permute-start.8 = (bf16[2,7168]{1,0:T(2,128)(2,1)S(1)}, bf16[2,7168]{1,0:T(2,128)(2,1)S(1)}, u32[]{:S(2)}, u32[]{:S(2)}) collective-permute-start(bf16[2,7168]{1,0:T(2,128)(2,1)S(1)} %get-tuple-element.39), channel_id=1, source_target_pairs={{0,10},{1,11},{2,8},{3,9},{4,14},{5,15},{6,12},{7,13},{8,2},{9,3},... | collective-permute-start | bytes 86024 | tf_op jit(solution)/shard_map/ppermute | solution.py:20
  15.1 3.3 %collective-permute-start.9 = (bf16[2,7168]{1,0:T(2,128)(2,1)S(1)}, bf16[2,7168]{1,0:T(2,128)(2,1)S(1)}, u32[]{:S(2)}, u32[]{:S(2)}) collective-permute-start(bf16[2,7168]{1,0:T(2,128)(2,1)S(1)} %get-tuple-element.40), channel_id=1, source_target_pairs={{0,9},{1,8},{2,11},{3,10},{4,13},{5,12},{6,15},{7,14},{8,1},{9,0},... | collective-permute-start | bytes 86024 | tf_op jit(solution)/shard_map/ppermute | solution.py:20
  18.4 4.2 %collective-permute-start.10 = (bf16[8,896]{1,0:T(8,128)(2,1)S(1)}, bf16[8,896]{1,0:T(8,128)(2,1)S(1)}, u32[]{:S(2)}, u32[]{:S(2)}) collective-permute-start(bf16[8,896]{1,0:T(8,128)(2,1)S(1)} %get-tuple-element.42), channel_id=1, source_target_pairs={{0,12},{1,13},{2,14},{3,15},{4,8},{5,9},{6,10},{7,11},{8,4},{9,5},... | collective-permute-start | bytes 43016 | tf_op jit(solution)/shard_map/ppermute | solution.py:20
